TPU v7x, 32 devices: a whole 2x2x4 slice. The times are simulated.
32 devices in a mesh: tp: 2 (over y), dp: 4 (over z), rep: 4 (over x, core).
Axes of the slice: x: 2, y: 2, z: 4, core: 2. Of those that a mesh axis runs over, the one named last changes fastest.
Arguments:
- layer_input: bfloat16 [16, 1024, 768], P(('dp', 'rep'), 'tp'), may hold values from -6 to 6
- history: bfloat16 [4, 16, 1024, 768], P(None, ('dp', 'rep'), 'tp'), may hold values from -6 to 6
- cotangent: bfloat16 [16, 1024, 768], P(('dp', 'rep'), 'tp'), may hold values from -6 to 6
- lengths: int32 [16, 3], P(('dp', 'rep')), may hold values from 1 to 512, 1024 in all within a row
- dwa_weights: float32 [5], replicated, may hold values from 0.2 to 1
- gain_one: float32 [768], replicated, may hold values from 0.1 to 1.9
- bias_one: float32 [768], replicated, may hold values from -3 to 3
- w_qkv: bfloat16 [3, 768, 768], P(None, None, 'tp'), may hold values from -0.21875 to 0.21875
- w_out: bfloat16 [768, 768], P('tp'), may hold values from -1.75 to 1.75
- gain_two: float32 [768], replicated, may hold values from 0.1 to 1.9
- bias_two: float32 [768], replicated, may hold values from -3 to 3
- w_up: bfloat16 [768, 3072], P(None, 'tp'), may hold values from -0.21875 to 0.21875
- w_down: bfloat16 [3072, 768], P('tp'), may hold values from -0.109375 to 0.109375
Outputs:
- output: bfloat16 [16, 1024, 768], P(('dp', 'rep'), 'tp')
- grad_input: bfloat16 [16, 1024, 768], P(('dp', 'rep'), 'tp')
- grad_history: bfloat16 [4, 16, 1024, 768], P(None, ('dp', 'rep'), 'tp')
- grad_dwa: float32 [5], replicated
- grad_gain_one: float32 [768], replicated
- grad_bias_one: float32 [768], replicated
- grad_w_qkv: float32 [3, 768, 768], P(None, 'dp', 'tp')
- grad_w_out: float32 [768, 768], P('tp', 'dp')
- grad_gain_two: float32 [768], replicated
- grad_bias_two: float32 [768], replicated
- grad_w_up: float32 [768, 3072], P('dp', 'tp')
- grad_w_down: float32 [3072, 768], P('tp', 'dp')
Inputs may be any that keep to these rules, and one draw needn't show every extreme that they name: Row g lists in order the lengths of the 3 sequences packed into group g; they sum to 1024 and the largest of each row is 512.
All inputs are finite; a program needn't handle non-finite values.
Results may differ from a plain program's by a relative error of at most 0.02.
Values may be sent and summed in bfloat16 or wider, within the bound.
No kernel may reach another device: no remote copies, remote signals or barrier semaphores. Data moves between devices by JAX's collectives and lax.ppermute only.
A program may use at most 128 MiB of HBM per device.

v0:
```python
from functools import partial
import math
import jax
import jax.numpy as jnp
from jax import lax
from jax.sharding import PartitionSpec as P

HEAD_DIM = 64
NEG_FILL = -1e30
NORM_EPS = 1e-05


def layer_norm(field, gain, shift):
    row_mean = jnp.mean(field, axis=-1, keepdims=True)
    centered = field - row_mean
    variance = jnp.mean(centered * centered, axis=-1, keepdims=True)
    return centered * lax.rsqrt(variance + NORM_EPS) * gain + shift


def positions(seq_lengths, token_count):
    seq_ends = jnp.cumsum(seq_lengths)
    seq_starts = seq_ends - seq_lengths
    token_index = jnp.arange(token_count, dtype=jnp.int32)
    seq_owner = jnp.sum((token_index[:, None] >= seq_ends[None, :]).astype(jnp.int32), axis=1)
    picked = (
        seq_owner[:, None] == jnp.arange(seq_lengths.shape[0], dtype=jnp.int32)[None, :]
    ).astype(jnp.int32)
    seq_begin = jnp.sum(picked * seq_starts[None, :], axis=1)
    return (seq_owner, token_index - seq_begin)


def rotary(token_place, head_size):
    half_dim = head_size // 2
    frequency = jnp.exp(jnp.arange(half_dim, dtype=jnp.float32) * (-math.log(10000.0) / half_dim))
    angles = token_place.astype(jnp.float32)[:, None] * frequency[None, :]
    return (jnp.cos(angles), jnp.sin(angles))


def rotate(field, cos_table, sin_table):
    half_dim = field.shape[-1] // 2
    first_half = field[..., :half_dim]
    second_half = field[..., half_dim:]
    cos_rows = cos_table[:, None, :]
    sin_rows = sin_table[:, None, :]
    return jnp.concatenate(
        [
            first_half * cos_rows - second_half * sin_rows,
            second_half * cos_rows + first_half * sin_rows,
        ],
        axis=-1,
    )


def rotate_back(field, cos_table, sin_table):
    half_dim = field.shape[-1] // 2
    first_half = field[..., :half_dim]
    second_half = field[..., half_dim:]
    cos_rows = cos_table[:, None, :]
    sin_rows = sin_table[:, None, :]
    return jnp.concatenate(
        [
            first_half * cos_rows + second_half * sin_rows,
            second_half * cos_rows - first_half * sin_rows,
        ],
        axis=-1,
    )


AXES = ("tp", "dp", "rep")


def pairs_of(move):
    tps, dps, reps = (lax.axis_size(name) for name in AXES)
    return [
        ((t * dps + d) * reps + r, (a * dps + b) * reps + e)
        for t in range(tps)
        for d in range(dps)
        for r in range(reps)
        for a, b, e in [move(t, d, r)]
    ]


def swap_diagonal(field):
    return lax.ppermute(field, AXES, pairs_of(lambda t, d, r: (r % 2, d, r - r % 2 + t)))


def swap_near(field):
    return lax.ppermute(field, "rep", [(r, r ^ 1) for r in range(lax.axis_size("rep"))])


def swap_far(field):
    return lax.ppermute(field, "rep", [(r, r ^ 2) for r in range(lax.axis_size("rep"))])


def ordered(own, other, first):
    return jnp.where(
        first, jnp.concatenate([own, other], axis=0), jnp.concatenate([other, own], axis=0)
    )


def reduce_pieces(pieces, near, far):
    dps = lax.axis_size("dp")
    mine = lax.dynamic_slice_in_dim(pieces, 2 * far, 2, 0)
    theirs = lax.dynamic_slice_in_dim(pieces, 2 - 2 * far, 2, 0)
    pair = mine.astype(jnp.float32) + swap_far(theirs).astype(jnp.float32)
    pair = swap_diagonal(pair.astype(jnp.bfloat16))
    mine = lax.dynamic_index_in_dim(pair, near, 0, keepdims=False)
    theirs = lax.dynamic_index_in_dim(pair, 1 - near, 0, keepdims=False)
    one = mine.astype(jnp.float32) + swap_near(theirs).astype(jnp.float32)
    rows = one.shape[0] // dps
    if dps <= 8:
        place = lax.axis_index("dp")
        total = lax.dynamic_slice_in_dim(one, place * rows, rows, 0)
        low = one.astype(jnp.bfloat16)
        for step in range(1, dps):
            target = lax.rem(place + step, dps)
            sent = lax.dynamic_slice_in_dim(low, target * rows, rows, 0)
            total = total + lax.ppermute(
                sent, "dp", [(d, (d + step) % dps) for d in range(dps)]
            ).astype(jnp.float32)
    else:
        total = lax.psum_scatter(one.astype(jnp.bfloat16), "dp", scatter_dimension=0, tiled=True)
    total = total.astype(jnp.bfloat16)[None]
    total = ordered(total, swap_near(total), near == 0)
    total = ordered(total, swap_far(total), far == 0)
    return total.astype(jnp.float32)


def local(
    layer_input,
    history,
    cotangent,
    lengths,
    dwa_weights,
    gain_one,
    bias_one,
    w_qkv,
    w_out,
    gain_two,
    bias_two,
    w_up,
    w_down,
):
    rows = layer_input.shape[1]
    whole = rows * lax.axis_size("tp")
    heads_here = w_qkv.shape[2] // HEAD_DIM
    hist_count = history.shape[0]
    part, slot = (lax.axis_index("tp"), lax.axis_index("rep"))
    near, far = (slot % 2, slot // 2)
    input_half = swap_diagonal(layer_input[0])
    w_qkv = swap_diagonal(w_qkv)
    cot_half = swap_diagonal(cotangent[0])
    w_out = swap_diagonal(w_out)
    w_up = swap_diagonal(w_up)
    w_down = swap_diagonal(w_down)
    own_lengths = jnp.where(near == part, lengths, swap_near(lengths))
    seq_owner, token_place = positions(own_lengths[0], whole)
    cos_table, sin_table = rotary(token_place, HEAD_DIM)
    block_rows = min(512, whole)
    block_starts = jnp.arange(whole // block_rows, dtype=jnp.int32) * block_rows
    key_index = jnp.arange(whole, dtype=jnp.int32)
    score_scale = HEAD_DIM ** (-0.5)
    layer_rows = ordered(input_half, swap_near(input_half), near == 0).astype(jnp.float32)
    norm_one = layer_norm(layer_rows, gain_one, bias_one).astype(jnp.bfloat16)
    qkv = jnp.einsum("td,cde->cte", norm_one, w_qkv, preferred_element_type=jnp.float32)
    shaped = qkv.reshape(3, whole, heads_here, HEAD_DIM)
    queries = rotate(shaped[0], cos_table, sin_table).astype(jnp.bfloat16)
    keys_rot = rotate(shaped[1], cos_table, sin_table).astype(jnp.bfloat16)
    values = shaped[2].astype(jnp.bfloat16)

    def scores_for(row_start):
        query_block = lax.dynamic_slice_in_dim(queries, row_start, block_rows, 0)
        rows_here = row_start + jnp.arange(block_rows, dtype=jnp.int32)
        owner_rows = lax.dynamic_slice_in_dim(seq_owner, row_start, block_rows, 0)
        allowed = (owner_rows[:, None] == seq_owner[None, :]) & (
            key_index[None, :] <= rows_here[:, None]
        )
        raw_scores = score_scale * jnp.einsum(
            "qhe,khe->hqk", query_block, keys_rot, preferred_element_type=jnp.float32
        )
        return (query_block, jnp.where(allowed[None], raw_scores, NEG_FILL))

    def attend(row_start):
        query_block, scores = scores_for(row_start)
        row_max = jnp.max(scores, axis=-1, keepdims=True)
        exponent = jnp.exp(scores - row_max)
        row_sum = jnp.sum(exponent, axis=-1, keepdims=True)
        probabilities = (exponent / row_sum).astype(jnp.bfloat16)
        mixed_block = jnp.einsum(
            "hqk,khe->qhe", probabilities, values, preferred_element_type=jnp.float32
        )
        return (
            mixed_block.reshape(block_rows, -1).astype(jnp.bfloat16),
            (row_max + jnp.log(row_sum))[..., 0],
        )

    mixed_blocks, log_sums = lax.map(attend, block_starts)
    mixed = mixed_blocks.reshape(whole, -1)
    attn = jnp.dot(mixed, w_out, preferred_element_type=jnp.float32).astype(jnp.bfloat16)
    attn = attn.astype(jnp.float32) + swap_near(attn).astype(jnp.float32)
    resid = layer_rows + attn
    norm_two = layer_norm(resid, gain_two, bias_two).astype(jnp.bfloat16)
    up_rows = jnp.dot(norm_two, w_up, preferred_element_type=jnp.float32)
    act = jax.nn.gelu(up_rows, approximate=True).astype(jnp.bfloat16)
    cot_rows = ordered(cot_half, swap_near(cot_half), near == 0)
    grad_block = dwa_weights[hist_count] * cot_rows.astype(jnp.float32)
    grad_down = grad_block.astype(jnp.bfloat16)
    grad_act = jnp.einsum("td,fd->tf", grad_down, w_down, preferred_element_type=jnp.float32)
    unused_gelu, gelu_pull = jax.vjp(partial(jax.nn.gelu, approximate=True), up_rows)
    grad_up = gelu_pull(grad_act)[0].astype(jnp.bfloat16)
    grad_norm_two = jnp.einsum("tf,df->td", grad_up, w_up, preferred_element_type=jnp.float32)
    grad_norm_two = grad_norm_two.astype(jnp.bfloat16)
    grad_norm_two = grad_norm_two.astype(jnp.float32) + swap_near(grad_norm_two).astype(jnp.float32)
    quarter = w_up.shape[1] // 4
    grad_w_down = jnp.einsum("td,tf->df", grad_down, act, preferred_element_type=jnp.float32)
    grad_w_down = grad_w_down.astype(jnp.bfloat16).reshape(-1, 4, quarter).transpose(1, 0, 2)
    grad_w_up = jnp.einsum("td,tf->df", norm_two, grad_up, preferred_element_type=jnp.float32)
    grad_w_up = grad_w_up.astype(jnp.bfloat16).reshape(-1, 4, quarter).transpose(1, 0, 2)
    grad_w_down = reduce_pieces(grad_w_down, near, far)
    grad_w_up = reduce_pieces(grad_w_up, near, far)
    down = jnp.dot(act, w_down, preferred_element_type=jnp.float32)
    down_mine = lax.dynamic_slice_in_dim(down, near * rows, rows, 0)
    down_theirs = lax.dynamic_slice_in_dim(down, (1 - near) * rows, rows, 0).astype(jnp.bfloat16)
    block_half = (
        lax.dynamic_slice_in_dim(resid, near * rows, rows, 0)
        + down_mine
        + swap_near(down_theirs).astype(jnp.float32)
    )
    block_out = swap_diagonal(block_half.astype(jnp.bfloat16)).astype(jnp.float32)
    hist_rows = history[:, 0].astype(jnp.float32)
    output = (
        jnp.sum(dwa_weights[:hist_count, None, None] * hist_rows, axis=0)
        + dwa_weights[hist_count] * block_out
    )
    grad_out = cotangent[0].astype(jnp.float32)
    grad_history = (dwa_weights[:hist_count, None, None] * grad_out[None]).astype(jnp.bfloat16)[
        :, None
    ]
    dwa_terms = jnp.concatenate(
        [jnp.sum(hist_rows * grad_out[None], axis=(1, 2)), jnp.sum(block_out * grad_out)[None]]
    )

    def layer_norm_back(field, gain, shift, grad, row_start):
        centered = field - jnp.mean(field, axis=-1, keepdims=True)
        scale = lax.rsqrt(jnp.mean(centered * centered, axis=-1, keepdims=True) + NORM_EPS)
        unit = centered * scale
        inner = grad * gain
        back = scale * (
            inner
            - jnp.mean(inner, axis=-1, keepdims=True)
            - unit * jnp.mean(inner * unit, axis=-1, keepdims=True)
        )
        half_grad = lax.dynamic_slice_in_dim(grad, row_start, rows, 0)
        half_unit = lax.dynamic_slice_in_dim(unit, row_start, rows, 0)
        return (back, jnp.sum(half_grad * half_unit, axis=0), jnp.sum(half_grad, axis=0))

    grad_resid_norm, grad_gain_two, grad_bias_two = layer_norm_back(
        resid, gain_two, bias_two, grad_norm_two, near * rows
    )
    grad_resid = grad_block + grad_resid_norm
    grad_attn = grad_resid.astype(jnp.bfloat16)
    grad_w_out = jnp.einsum("td,te->de", grad_attn, mixed, preferred_element_type=jnp.float32)
    grad_mixed = jnp.einsum(
        "td,ed->te", grad_attn, w_out, preferred_element_type=jnp.float32
    ).astype(jnp.bfloat16)
    grad_mixed = grad_mixed.reshape(whole, heads_here, HEAD_DIM)

    def attend_back(carry, item):
        grad_keys, grad_values = carry
        row_start, log_sum = item
        query_block, scores = scores_for(row_start)
        probabilities = jnp.exp(scores - log_sum[..., None])
        probs_low = probabilities.astype(jnp.bfloat16)
        grad_block_rows = lax.dynamic_slice_in_dim(grad_mixed, row_start, block_rows, 0)
        grad_values = grad_values + jnp.einsum(
            "hqk,qhe->khe", probs_low, grad_block_rows, preferred_element_type=jnp.float32
        )
        grad_probs = jnp.einsum(
            "qhe,khe->hqk", grad_block_rows, values, preferred_element_type=jnp.float32
        )
        row_dot = jnp.sum(probabilities * grad_probs, axis=-1, keepdims=True)
        grad_scores = (probabilities * (grad_probs - row_dot)).astype(jnp.bfloat16)
        grad_queries = score_scale * jnp.einsum(
            "hqk,khe->qhe", grad_scores, keys_rot, preferred_element_type=jnp.float32
        )
        grad_keys = grad_keys + score_scale * jnp.einsum(
            "hqk,qhe->khe", grad_scores, query_block, preferred_element_type=jnp.float32
        )
        return ((grad_keys, grad_values), grad_queries)

    zero_heads = jnp.zeros((whole, heads_here, HEAD_DIM), jnp.float32)
    (grad_keys, grad_values), grad_query_blocks = lax.scan(
        attend_back, (zero_heads, zero_heads), (block_starts, log_sums)
    )
    grad_queries = grad_query_blocks.reshape(whole, heads_here, HEAD_DIM)
    grad_qkv = jnp.stack(
        [
            rotate_back(grad_queries, cos_table, sin_table),
            rotate_back(grad_keys, cos_table, sin_table),
            grad_values,
        ]
    )
    grad_qkv = grad_qkv.reshape(3, whole, heads_here * HEAD_DIM).astype(jnp.bfloat16)
    grad_w_qkv = jnp.einsum("td,cte->cde", norm_one, grad_qkv, preferred_element_type=jnp.float32)
    grad_w_attn = reduce_pieces(
        jnp.concatenate([grad_w_qkv, grad_w_out[None]], axis=0).astype(jnp.bfloat16), near, far
    )
    grad_norm_one = jnp.einsum("cte,cde->td", grad_qkv, w_qkv, preferred_element_type=jnp.float32)
    one_mine = lax.dynamic_slice_in_dim(grad_norm_one, near * rows, rows, 0)
    one_theirs = lax.dynamic_slice_in_dim(grad_norm_one, (1 - near) * rows, rows, 0)
    grad_norm_half = one_mine + swap_near(one_theirs.astype(jnp.bfloat16)).astype(jnp.float32)
    grad_rows_norm, grad_gain_one, grad_bias_one = layer_norm_back(
        input_half.astype(jnp.float32), gain_one, bias_one, grad_norm_half, 0
    )
    grad_resid_half = lax.dynamic_slice_in_dim(grad_resid, near * rows, rows, 0)
    grad_input = swap_diagonal((grad_resid_half + grad_rows_norm).astype(jnp.bfloat16))
    small_sums = lax.psum(
        (grad_gain_one, grad_bias_one, grad_gain_two, grad_bias_two, dwa_terms), AXES
    )
    return (
        output.astype(jnp.bfloat16)[None],
        grad_input[None],
        grad_history,
        small_sums[4],
        small_sums[0],
        small_sums[1],
        grad_w_attn[:3],
        grad_w_attn[3].T,
        small_sums[2],
        small_sums[3],
        grad_w_up.transpose(1, 0, 2).reshape(grad_w_up.shape[1], -1),
        grad_w_down.transpose(1, 0, 2).reshape(grad_w_down.shape[1], -1).T,
    )


def solution(mesh):
    in_specs = (
        P(("dp", "rep"), "tp", None),
        P(None, ("dp", "rep"), "tp", None),
        P(("dp", "rep"), "tp", None),
        P(("dp", "rep"), None),
        P(),
        P(),
        P(),
        P(None, None, "tp"),
        P("tp", None),
        P(),
        P(),
        P(None, "tp"),
        P("tp", None),
    )
    out_specs = (
        P(("dp", "rep"), "tp", None),
        P(("dp", "rep"), "tp", None),
        P(None, ("dp", "rep"), "tp", None),
        P(),
        P(),
        P(),
        P(None, "dp", "tp"),
        P("tp", "dp"),
        P(),
        P(),
        P("dp", "tp"),
        P("tp", "dp"),
    )
    return jax.shard_map(local, mesh=mesh, in_specs=in_specs, out_specs=out_specs, check_vma=False)
```

profile of v0, /device:TPU:0, one launch (start us, length us, event | category | flops | bytes accessed | tf_op | source)
XLA Modules:
  0.0 490.6 jit_solution(10900318988023599955)
XLA Ops:
  8.1 6.0 %collective-permute-start.4 = (bf16[384,768]{1,0:T(8,128)(2,1)}, bf16[384,768]{1,0:T(8,128)(2,1)}, u32[]{:S(2)}, u32[]{:S(2)}) collective-permute-start(bf16[384,768]{1,0:T(8,128)(2,1)} %param.25), channel_id=1, source_target_pairs={{0,0},{1,16},{2,2},{3,18},{4,4},{5,20},{6,6},{7,22},{8,8},{9,24},{... | collective-permute-start | bytes 1769480 | tf_op jit(solution)/shard_map/ppermute | solution.py:84
  16.4 7.6 %collective-permute-start.10 = (bf16[512,768]{0,1:T(8,128)(2,1)}, bf16[512,768]{0,1:T(8,128)(2,1)}, u32[]{:S(2)}, u32[]{:S(2)}) collective-permute-start(bf16[512,768]{0,1:T(8,128)(2,1)} %bitcast.14), channel_id=1, source_target_pairs={{0,0},{1,16},{2,2},{3,18},{4,4},{5,20},{6,6},{7,22},{8,8},{9,24},{... | collective-permute-start | bytes 2359304 | tf_op jit(solution)/shard_map/ppermute | solution.py:84
  28.4 19.2 %collective-permute-start.6 = (bf16[768,1536]{1,0:T(8,128)(2,1)}, bf16[768,1536]{1,0:T(8,128)(2,1)}, u32[]{:S(2)}, u32[]{:S(2)}) collective-permute-start(bf16[768,1536]{1,0:T(8,128)(2,1)} %param.28), channel_id=1, source_target_pairs={{0,0},{1,16},{2,2},{3,18},{4,4},{5,20},{6,6},{7,22},{8,8},{9,24},{... | collective-permute-start | bytes 7077896 | tf_op jit(solution)/shard_map/ppermute | solution.py:84
  50.3 19.8 %collective-permute-start.7 = (bf16[1536,768]{1,0:T(8,128)(2,1)}, bf16[1536,768]{1,0:T(8,128)(2,1)}, u32[]{:S(2)}, u32[]{:S(2)}) collective-permute-start(bf16[1536,768]{1,0:T(8,128)(2,1)} %param.29), channel_id=1, source_target_pairs={{0,0},{1,16},{2,2},{3,18},{4,4},{5,20},{6,6},{7,22},{8,8},{9,24},{... | collective-permute-start | bytes 7077896 | tf_op jit(solution)/shard_map/ppermute | solution.py:84
  76.4 35.5 %while.28 = (s32[]{:T(128)}, bf16[2,512,384]{2,1,0:T(8,128)(2,1)}, f32[2,6,512]{2,1,0:T(8,128)S(1)}, s32[2]{0:T(128)S(1)}, s32[1024]{0:T(1024)S(1)}, /*index=5*/...) while((s32[]{:T(128)}, bf16[2,512,384]{2,1,0:T(8,128)(2,1)}, ...), condition=%wide.region_9.10_spmd.clone, body=%wide.region_6.9_spmd.clone.sunk | while | flops 844822016 | bytes 50194668 | solution.py:197
  87.8 5.1 %fusion.140 = bf16[6,512,64]{1,2,0:T(8,128)(2,1)S(1)} fusion(bf16[1024,6,64]{0,2,1:T(8,128)(2,1)} %get-tuple-element.482, f32[6,512,1024]{2,1,0:T(8,128)S(1)} %get-tuple-element.438, f32[6,512]{1,0:T(8,128)S(1)} %fusion.139, f32[6,512]{1,0:T(8,128)S(1)} %get-tuple-element.439, pred[512,1024]{1,0:T(8,128)(4,1)S(1)} %fusion.137), kind=kOutput, calls=%fused_computation.10.clone.1 | convolution fusion | flops 418578432 | bytes 14311424 | tf_op jit(solution)/shard_map/while/body/eval_jaxpr/hqk,khe->qhe/dot_general | solution.py:189
  105.5 5.1 %fusion.140 = bf16[6,512,64]{1,2,0:T(8,128)(2,1)S(1)} fusion(bf16[1024,6,64]{0,2,1:T(8,128)(2,1)} %get-tuple-element.482, f32[6,512,1024]{2,1,0:T(8,128)S(1)} %get-tuple-element.438, f32[6,512]{1,0:T(8,128)S(1)} %fusion.139, f32[6,512]{1,0:T(8,128)S(1)} %get-tuple-element.439, pred[512,1024]{1,0:T(8,128)(4,1)S(1)} %fusion.137), kind=kOutput, calls=%fused_computation.10.clone.1 | convolution fusion | flops 418578432 | bytes 14311424 | tf_op jit(solution)/shard_map/while/body/eval_jaxpr/hqk,khe->qhe/dot_general | solution.py:189
  119.8 5.2 %fusion.35 = (f32[4]{0:T(128)}, f32[512,768]{1,0:T(8,128)}) fusion(bf16[4,1,512,768]{3,2,1,0:T(8,128)(2,1)} %param.18, f32[512,768]{1,0:T(8,128)S(1)} %copy.124, f32[4]{0:T(128)S(1)} %bitcast.181), kind=kLoop, calls=%fused_computation.50 | loop fusion | flops 7471100 | bytes 6291488 | tf_op jit(solution)/shard_map/reduce_sum | solution.py:240
  137.8 5.8 %fusion.91 = f32[1024,1536]{1,0:T(8,128)S(1)} fusion(bf16[768,1536]{1,0:T(8,128)(2,1)} %collective-permute-done.6, f32[1024,768]{0,1:T(8,128)S(1)} %subtract_multiply_fusion, f32[768]{0:T(1024)S(1)} %copy-done.41, f32[768]{0:T(1024)S(1)} %copy-done.30), kind=kOutput, calls=%fused_computation.206 | convolution fusion | flops 2418278400 | bytes 11802624 | tf_op jit(solution)/shard_map/dot_general | solution.py:203
  146.5 7.0 %convolution_convert_fusion = bf16[768,1536]{1,0:T(8,128)(2,1)} fusion(f32[]{:T(128)} %bitcast.1, bf16[512,768]{0,1:T(8,128)(2,1)S(1)} %collective-permute-done.11, bf16[512,768]{0,1:T(8,128)(2,1)} %collective-permute-done.10, pred[]{:T(512)S(6)} %eq.64, f32[1024,1536]{1,0:T(8,128)S(1)} %fusion.91), kind=kOutput, calls=%fused_computation.65 | convolution fusion | flops 2440691712 | bytes 10223621 | tf_op jit(solution)/shard_map/td,tf->df/dot_general | solution.py:215
  161.9 10.7 %fusion.42 = bf16[1024,1536]{1,0:T(8,128)(2,1)S(1)} fusion(f32[1024,1536]{1,0:T(8,128)} %copy-done.44, bf16[1536,768]{1,0:T(8,128)(2,1)} %collective-permute-done.7, f32[]{:T(128)} %bitcast.1, bf16[512,768]{0,1:T(8,128)(2,1)S(1)} %copy-done.25, bf16[512,768]{0,1:T(8,128)(2,1)} %collective-permute-done.10, pred[]{:T(512)S(6)} %eq.64), kind=kOutput, calls=%fused_computation.57 | convolution fusion | flops 2456813568 | bytes 13369349 | tf_op jit(solution)/shard_map/td,fd->tf/dot_general | solution.py:208
  172.6 5.5 %convolution_convert_fusion.3 = bf16[1024,768]{0,1:T(8,128)(2,1)} fusion(bf16[1024,1536]{1,0:T(8,128)(2,1)S(1)} %fusion.42, bf16[768,1536]{1,0:T(8,128)(2,1)} %collective-permute-done.6), kind=kOutput, calls=%fused_computation.103 | convolution fusion | flops 2416705536 | bytes 7077888 | tf_op jit(solution)/shard_map/tf,df->td/dot_general | solution.py:211
  178.1 5.0 %fusion.92 = f32[1024,768]{0,1:T(8,128)S(1)} fusion(bf16[1536,768]{1,0:T(8,128)(2,1)} %collective-permute-done.7, f32[1024,1536]{1,0:T(8,128)S(1)} %bitcast.184), kind=kOutput, calls=%fused_computation.207 | convolution fusion | flops 2430074880 | bytes 11796480 | tf_op jit(solution)/shard_map/dot_general | solution.py:221
  201.0 7.6 %collective-permute-start.9 = (bf16[512,768]{0,1:T(8,128)(2,1)}, bf16[512,768]{0,1:T(8,128)(2,1)}, u32[]{:S(2)}, u32[]{:S(2)}) collective-permute-start(bf16[512,768]{0,1:T(8,128)(2,1)} %add_convert_fusion.2), channel_id=1, source_target_pairs={{0,0},{1,16},{2,2},{3,18},{4,4},{5,20},{6,6},{7,22},{8,8},{9,24},{... | collective-permute-start | bytes 2359304 | tf_op jit(solution)/shard_map/ppermute | solution.py:84
  208.6 4.5 multiply_reduce_fusion.3
  213.1 4.9 multiply_add_fusion
  222.5 97.3 %while.29 = (s32[]{:T(128)}, f32[1024,6,64]{0,2,1:T(8,128)S(1)}, f32[1024,6,64]{0,2,1:T(8,128)}, f32[2,512,6,64]{1,0,3,2:T(2,128)}, s32[2]{0:T(128)S(1)}, /*inde...) while((s32[]{:T(128)}, f32[1024,6,64]{0,2,1:T(8,128)S(1)}, ...), condition=%wide.region_18.19_spmd.clone, body=%wide.region_16.18_spmd.clone.sunk | while | flops 2064184832 | bytes 110725352 | solution.py:292
  229.8 5.6 %bitcast_add_fusion.7 = f32[1024,6,64]{0,2,1:T(8,128)} fusion(f32[1024,6,64]{0,2,1:T(8,128)} %get-tuple-element.502, f32[6,512,1024]{2,1,0:T(8,128)S(1)} %fusion.150, f32[6,512]{1,0:T(8,128)S(1)} %dynamic-slice_bitcast_fusion.7, pred[512,1024]{1,0:T(8,128)(4,1)S(1)} %fusion.151, pred[]{:T(512)S(6)} %compare.9, ...), kind=kOutput, calls=%fused_computation.27.clone.1 | convolution fusion | flops 416022528 | bytes 16658437 | tf_op jit(solution)/shard_map/while/body/eval_jaxpr/hqk,qhe->khe/dot_general | solution.py:275
  235.4 8.5 %multiply_reduce_fusion.7 = (f32[6,512]{1,0:T(8,128)S(1)}, f32[6,512,1024]{2,1,0:T(8,128)}) fusion(f32[6,512,1024]{2,1,0:T(8,128)S(1)} %fusion.150, f32[6,512]{1,0:T(8,128)S(1)} %dynamic-slice_bitcast_fusion.7, pred[512,1024]{1,0:T(8,128)(4,1)S(1)} %fusion.151, bf16[1024,6,64]{0,2,1:T(8,128)(2,1)} %get-tuple-element.524, ...), kind=kOutput, calls=%fused_computation.20.clone.1 | convolution fusion | flops 418378752 | bytes 26894340 | tf_op jit(solution)/shard_map/while/body/eval_jaxpr/qhe,khe->hqk/dot_general | solution.py:278
  243.9 6.9 %multiply_convert_fusion.6 = bf16[6,512,1024]{2,1,0:T(8,128)(2,1)S(1)} fusion(f32[6,512,1024]{2,1,0:T(8,128)} %get-tuple-element.451, f32[6,512,1024]{2,1,0:T(8,128)S(1)} %fusion.150, f32[6,512]{1,0:T(8,128)S(1)} %get-tuple-element.452, f32[6,512]{1,0:T(8,128)S(1)} %dynamic-slice_bitcast_fusion.7, pred[512,1024]{1,0:T(8,128)(4,1)S(1)} %fusion.151), kind=kLoop, calls=%fused_computation.19.clone.1 | loop fusion | flops 18874368 | bytes 32006144 | tf_op jit(solution)/shard_map/while/body/eval_jaxpr/convert_element_type | solution.py:282
  256.1 14.9 %dynamic_update_slice.22 = f32[2,512,6,64]{1,0,3,2:T(2,128)} dynamic-update-slice(f32[2,512,6,64]{1,0,3,2:T(2,128)} %get-tuple-element.503, f32[1,512,6,64]{1,0,3,2:T(1,128)S(1)} %copy.173, s32[]{:T(128)S(6)} %copy.190, s32[]{:T(128)} %constant.132.clone.1..sunk.1, s32[]{:T(128)} %constant.132.clone.1..sunk.1, s32[]{:T(128)} %constant.132.clone.1..sunk.1) | dynamic-update-slice | bytes 1572868 | tf_op jit(solution)/shard_map/while/body/jit(dynamic_update_index_in_dim)/dynamic_update_slice | solution.py:292
  278.0 6.1 %bitcast_add_fusion.7 = f32[1024,6,64]{0,2,1:T(8,128)} fusion(f32[1024,6,64]{0,2,1:T(8,128)} %get-tuple-element.502, f32[6,512,1024]{2,1,0:T(8,128)S(1)} %fusion.150, f32[6,512]{1,0:T(8,128)S(1)} %dynamic-slice_bitcast_fusion.7, pred[512,1024]{1,0:T(8,128)(4,1)S(1)} %fusion.151, pred[]{:T(512)S(6)} %compare.9, ...), kind=kOutput, calls=%fused_computation.27.clone.1 | convolution fusion | flops 416022528 | bytes 16658437 | tf_op jit(solution)/shard_map/while/body/eval_jaxpr/hqk,qhe->khe/dot_general | solution.py:275
  284.1 8.5 %multiply_reduce_fusion.7 = (f32[6,512]{1,0:T(8,128)S(1)}, f32[6,512,1024]{2,1,0:T(8,128)}) fusion(f32[6,512,1024]{2,1,0:T(8,128)S(1)} %fusion.150, f32[6,512]{1,0:T(8,128)S(1)} %dynamic-slice_bitcast_fusion.7, pred[512,1024]{1,0:T(8,128)(4,1)S(1)} %fusion.151, bf16[1024,6,64]{0,2,1:T(8,128)(2,1)} %get-tuple-element.524, ...), kind=kOutput, calls=%fused_computation.20.clone.1 | convolution fusion | flops 418378752 | bytes 26894340 | tf_op jit(solution)/shard_map/while/body/eval_jaxpr/qhe,khe->hqk/dot_general | solution.py:278
  292.6 6.9 %multiply_convert_fusion.6 = bf16[6,512,1024]{2,1,0:T(8,128)(2,1)S(1)} fusion(f32[6,512,1024]{2,1,0:T(8,128)} %get-tuple-element.451, f32[6,512,1024]{2,1,0:T(8,128)S(1)} %fusion.150, f32[6,512]{1,0:T(8,128)S(1)} %get-tuple-element.452, f32[6,512]{1,0:T(8,128)S(1)} %dynamic-slice_bitcast_fusion.7, pred[512,1024]{1,0:T(8,128)(4,1)S(1)} %fusion.151), kind=kLoop, calls=%fused_computation.19.clone.1 | loop fusion | flops 18874368 | bytes 32006144 | tf_op jit(solution)/shard_map/while/body/eval_jaxpr/convert_element_type | solution.py:282
  304.8 14.9 %dynamic_update_slice.22 = f32[2,512,6,64]{1,0,3,2:T(2,128)} dynamic-update-slice(f32[2,512,6,64]{1,0,3,2:T(2,128)} %get-tuple-element.503, f32[1,512,6,64]{1,0,3,2:T(1,128)S(1)} %copy.173, s32[]{:T(128)S(6)} %copy.190, s32[]{:T(128)} %constant.132.clone.1..sunk.1, s32[]{:T(128)} %constant.132.clone.1..sunk.1, s32[]{:T(128)} %constant.132.clone.1..sunk.1) | dynamic-update-slice | bytes 1572868 | tf_op jit(solution)/shard_map/while/body/jit(dynamic_update_index_in_dim)/dynamic_update_slice | solution.py:292
  347.5 16.8 %collective-permute-done.15 = bf16[2,768,384]{1,2,0:T(8,128)(2,1)S(1)} collective-permute-done((bf16[2,768,384]{1,2,0:T(8,128)(2,1)S(1)}, bf16[2,768,384]{1,2,0:T(8,128)(2,1)S(1)}, u32[]{:S(2)}, u32[]{:S(2)}) %collective-permute-start.15) | collective-permute-done | bytes 1179680 | tf_op jit(solution)/shard_map/ppermute | solution.py:92
  378.2 6.9 %collective-permute-start.17 = (bf16[768,384]{0,1:T(8,128)(2,1)S(1)}, bf16[768,384]{0,1:T(8,128)(2,1)S(1)}, u32[]{:S(2)}, u32[]{:S(2)}) collective-permute-start(bf16[768,384]{0,1:T(8,128)(2,1)S(1)} %dynamic-slice_bitcast_fusion.5), channel_id=1, source_target_pairs={{0,1},{1,0},{2,3},{3,2},{4,5},{5,4},{6,7},{7,6},{8,9},{9,8},{10,11... | collective-permute-start | bytes 1769480 | tf_op jit(solution)/shard_map/ppermute | solution.py:88
  389.5 9.9 %collective-permute-done.35 = bf16[192,384]{0,1:T(8,128)(2,1)S(1)} collective-permute-done((bf16[192,384]{0,1:T(8,128)(2,1)S(1)}, bf16[192,384]{0,1:T(8,128)(2,1)S(1)}, u32[]{:S(2)}, u32[]{:S(2)}) %collective-permute-start.35) | collective-permute-done | bytes 147488 | tf_op jit(solution)/shard_map/ppermute | solution.py:118
  400.2 6.3 %collective-permute-start.18 = (bf16[192,384]{0,1:T(8,128)(2,1)S(1)}, bf16[192,384]{0,1:T(8,128)(2,1)S(1)}, u32[]{:S(2)}, u32[]{:S(2)}) collective-permute-start(bf16[192,384]{0,1:T(8,128)(2,1)S(1)} %get-tuple-element.318), channel_id=1, source_target_pairs={{0,4},{4,8},{8,12},{12,0},{1,5},{5,9},{9,13},{13,1},{2,6},{6,10},{... | collective-permute-start | bytes 442376 | tf_op jit(solution)/shard_map/ppermute | solution.py:118
  406.5 9.8 %collective-permute-done.27 = bf16[192,384]{0,1:T(8,128)(2,1)S(1)} collective-permute-done((bf16[192,384]{0,1:T(8,128)(2,1)S(1)}, bf16[192,384]{0,1:T(8,128)(2,1)S(1)}, u32[]{:S(2)}, u32[]{:S(2)}) %collective-permute-start.27) | collective-permute-done | bytes 147488 | tf_op jit(solution)/shard_map/ppermute | solution.py:118
  420.4 8.5 %collective-permute-done.19 = bf16[192,384]{0,1:T(8,128)(2,1)S(1)} collective-permute-done((bf16[192,384]{0,1:T(8,128)(2,1)S(1)}, bf16[192,384]{0,1:T(8,128)(2,1)S(1)}, u32[]{:S(2)}, u32[]{:S(2)}) %collective-permute-start.19) | collective-permute-done | bytes 147488 | tf_op jit(solution)/shard_map/ppermute | solution.py:118
  432.2 42.3 %all-reduce = (f32[5]{0:T(128)}, f32[768]{0:T(1024)}, f32[768]{0:T(1024)}, f32[768]{0:T(1024)}, f32[768]{0:T(1024)}) all-reduce(f32[5]{0:T(128)S(1)} %pad_maximum_fusion.7, f32[768]{0:T(1024)S(1)} %get-tuple-element.239, f32[768]{0:T(1024)S(1)} %get-tuple-element.242, ...), channel_id=1, replica_groups=mesh['tp'=2,'dp'=4,'rep'=4] {'tp','dp','rep'}, use_global_device_ids=true, to_apply=%region_23.24 | all-reduce | flops 3077 | bytes 24616 | tf_op jit(solution)/shard_map/psum | solution.py:317
  (302 shorter events, 188.1 us)
Async XLA Ops:
  3.1 44.8 %collective-permute-start = (bf16[512,768]{0,1:T(8,128)(2,1)}, bf16[512,768]{0,1:T(8,128)(2,1)S(1)}, u32[]{:S(2)}, u32[]{:S(2)}) collective-permute-start(bf16[512,768]{0,1:T(8,128)(2,1)} %bitcast.177), channel_id=1, source_target_pairs={{0,0},{1,16},{2,2},{3,18},{4,4},{5,20},{6,6},{7,22},{8,8},{9,24},{... | collective-permute-start | bytes 2359304 | tf_op jit(solution)/shard_map/ppermute | solution.py:84
  4.9 23.5 %collective-permute-start.2 = (s32[1,3]{1,0:T(1,128)}, s32[1,3]{1,0:T(1,128)S(1)}, u32[]{:S(2)}, u32[]{:S(2)}) collective-permute-start(s32[1,3]{1,0:T(1,128)} %param.20), channel_id=1, source_target_pairs={{0,1},{1,0},{2,3},{3,2},{4,5},{5,4},{6,7},{7,6},{8,9},{9,8},{10,11... | collective-permute-start | bytes 44 | tf_op jit(solution)/shard_map/ppermute | solution.py:88
  8.1 103.8 %collective-permute-start.4 = (bf16[384,768]{1,0:T(8,128)(2,1)}, bf16[384,768]{1,0:T(8,128)(2,1)}, u32[]{:S(2)}, u32[]{:S(2)}) collective-permute-start(bf16[384,768]{1,0:T(8,128)(2,1)} %param.25), channel_id=1, source_target_pairs={{0,0},{1,16},{2,2},{3,18},{4,4},{5,20},{6,6},{7,22},{8,8},{9,24},{... | collective-permute-start | bytes 1769480 | tf_op jit(solution)/shard_map/ppermute | solution.py:84
  16.4 114.7 %collective-permute-start.10 = (bf16[512,768]{0,1:T(8,128)(2,1)}, bf16[512,768]{0,1:T(8,128)(2,1)}, u32[]{:S(2)}, u32[]{:S(2)}) collective-permute-start(bf16[512,768]{0,1:T(8,128)(2,1)} %bitcast.14), channel_id=1, source_target_pairs={{0,0},{1,16},{2,2},{3,18},{4,4},{5,20},{6,6},{7,22},{8,8},{9,24},{... | collective-permute-start | bytes 2359304 | tf_op jit(solution)/shard_map/ppermute | solution.py:84
  26.2 44.9 %collective-permute-start.3 = (bf16[3,768,384]{1,2,0:T(8,128)(2,1)}, bf16[3,768,384]{1,2,0:T(8,128)(2,1)S(1)}, u32[]{:S(2)}, u32[]{:S(2)}) collective-permute-start(bf16[3,768,384]{1,2,0:T(8,128)(2,1)} %copy.109), channel_id=1, source_target_pairs={{0,0},{1,16},{2,2},{3,18},{4,4},{5,20},{6,6},{7,22},{8,8},{9,24},{... | collective-permute-start | bytes 5308424 | tf_op jit(solution)/shard_map/ppermute | solution.py:84
  28.4 109.4 %collective-permute-start.6 = (bf16[768,1536]{1,0:T(8,128)(2,1)}, bf16[768,1536]{1,0:T(8,128)(2,1)}, u32[]{:S(2)}, u32[]{:S(2)}) collective-permute-start(bf16[768,1536]{1,0:T(8,128)(2,1)} %param.28), channel_id=1, source_target_pairs={{0,0},{1,16},{2,2},{3,18},{4,4},{5,20},{6,6},{7,22},{8,8},{9,24},{... | collective-permute-start | bytes 7077896 | tf_op jit(solution)/shard_map/ppermute | solution.py:84
  50.3 111.6 %collective-permute-start.7 = (bf16[1536,768]{1,0:T(8,128)(2,1)}, bf16[1536,768]{1,0:T(8,128)(2,1)}, u32[]{:S(2)}, u32[]{:S(2)}) collective-permute-start(bf16[1536,768]{1,0:T(8,128)(2,1)} %param.29), channel_id=1, source_target_pairs={{0,0},{1,16},{2,2},{3,18},{4,4},{5,20},{6,6},{7,22},{8,8},{9,24},{... | collective-permute-start | bytes 7077896 | tf_op jit(solution)/shard_map/ppermute | solution.py:84
  115.4 17.3 %collective-permute-start.5 = (bf16[1024,768]{0,1:T(8,128)(2,1)}, bf16[1024,768]{0,1:T(8,128)(2,1)}, u32[]{:S(2)}, u32[]{:S(2)}) collective-permute-start(bf16[1024,768]{0,1:T(8,128)(2,1)} %convolution_convert_fusion.2), channel_id=1, source_target_pairs={{0,1},{1,0},{2,3},{3,2},{4,5},{5,4},{6,7},{7,6},{8,9},{9,8},{10,11... | collective-permute-start | bytes 4718600 | tf_op jit(solution)/shard_map/ppermute | solution.py:88
  131.1 12.5 %collective-permute-start.11 = (bf16[512,768]{0,1:T(8,128)(2,1)}, bf16[512,768]{0,1:T(8,128)(2,1)S(1)}, u32[]{:S(2)}, u32[]{:S(2)}) collective-permute-start(bf16[512,768]{0,1:T(8,128)(2,1)} %collective-permute-done.10), channel_id=1, source_target_pairs={{0,1},{1,0},{2,3},{3,2},{4,5},{5,4},{6,7},{7,6},{8,9},{9,8},{10,11... | collective-permute-start | bytes 2359304 | tf_op jit(solution)/shard_map/ppermute | solution.py:88
  160.4 177.3 %collective-permute-start.31 = (bf16[2,768,384]{1,2,0:T(8,128)(2,1)}, bf16[2,768,384]{1,2,0:T(8,128)(2,1)}, u32[]{:S(2)}, u32[]{:S(2)}) collective-permute-start(bf16[2,768,384]{1,2,0:T(8,128)(2,1)} %dynamic-slice_bitcast_fusion.1), channel_id=1, source_target_pairs={{0,2},{1,3},{2,0},{3,1},{4,6},{5,7},{6,4},{7,5},{8,10},{9,11},{10,... | collective-permute-start | bytes 3538952 | tf_op jit(solution)/shard_map/ppermute | solution.py:92
  178.1 30.5 %collective-permute-start.12 = (bf16[1024,768]{0,1:T(8,128)(2,1)}, bf16[1024,768]{0,1:T(8,128)(2,1)}, u32[]{:S(2)}, u32[]{:S(2)}) collective-permute-start(bf16[1024,768]{0,1:T(8,128)(2,1)} %convolution_convert_fusion.3), channel_id=1, source_target_pairs={{0,1},{1,0},{2,3},{3,2},{4,5},{5,4},{6,7},{7,6},{8,9},{9,8},{10,11... | collective-permute-start | bytes 4718600 | tf_op jit(solution)/shard_map/ppermute | solution.py:88
  197.1 143.0 %collective-permute-start.23 = (bf16[2,768,384]{1,2,0:T(8,128)(2,1)}, bf16[2,768,384]{1,2,0:T(8,128)(2,1)}, u32[]{:S(2)}, u32[]{:S(2)}) collective-permute-start(bf16[2,768,384]{1,2,0:T(8,128)(2,1)} %dynamic-slice_bitcast_fusion.2), channel_id=1, source_target_pairs={{0,2},{1,3},{2,0},{3,1},{4,6},{5,7},{6,4},{7,5},{8,10},{9,11},{10,... | collective-permute-start | bytes 3538952 | tf_op jit(solution)/shard_map/ppermute | solution.py:92
  201.0 141.8 %collective-permute-start.9 = (bf16[512,768]{0,1:T(8,128)(2,1)}, bf16[512,768]{0,1:T(8,128)(2,1)}, u32[]{:S(2)}, u32[]{:S(2)}) collective-permute-start(bf16[512,768]{0,1:T(8,128)(2,1)} %add_convert_fusion.2), channel_id=1, source_target_pairs={{0,0},{1,16},{2,2},{3,18},{4,4},{5,20},{6,6},{7,22},{8,8},{9,24},{... | collective-permute-start | bytes 2359304 | tf_op jit(solution)/shard_map/ppermute | solution.py:84
  332.9 13.7 %collective-permute-start.13 = (bf16[512,768]{0,1:T(8,128)(2,1)S(1)}, bf16[512,768]{0,1:T(8,128)(2,1)S(1)}, u32[]{:S(2)}, u32[]{:S(2)}) collective-permute-start(bf16[512,768]{0,1:T(8,128)(2,1)S(1)} %dynamic-slice_convert_fusion), channel_id=1, source_target_pairs={{0,1},{1,0},{2,3},{3,2},{4,5},{5,4},{6,7},{7,6},{8,9},{9,8},{10,11... | collective-permute-start | bytes 2359304 | tf_op jit(solution)/shard_map/ppermute | solution.py:88
  336.2 28.2 %collective-permute-start.15 = (bf16[2,768,384]{1,2,0:T(8,128)(2,1)S(1)}, bf16[2,768,384]{1,2,0:T(8,128)(2,1)S(1)}, u32[]{:S(2)}, u32[]{:S(2)}) collective-permute-start(bf16[2,768,384]{1,2,0:T(8,128)(2,1)S(1)} %fusion.74), channel_id=1, source_target_pairs={{0,2},{1,3},{2,0},{3,1},{4,6},{5,7},{6,4},{7,5},{8,10},{9,11},{10,... | collective-permute-start | bytes 3538952 | tf_op jit(solution)/shard_map/ppermute | solution.py:92
  339.3 26.4 %collective-permute-start.32 = (bf16[2,768,384]{1,2,0:T(8,128)(2,1)S(1)}, bf16[2,768,384]{1,2,0:T(8,128)(2,1)S(1)}, u32[]{:S(2)}, u32[]{:S(2)}) collective-permute-start(bf16[2,768,384]{1,2,0:T(8,128)(2,1)S(1)} %fusion.50), channel_id=1, source_target_pairs={{0,0},{1,16},{2,2},{3,18},{4,4},{5,20},{6,6},{7,22},{8,8},{9,24},{... | collective-permute-start | bytes 3538952 | tf_op jit(solution)/shard_map/ppermute | solution.py:84
  341.8 25.0 %collective-permute-start.24 = (bf16[2,768,384]{1,2,0:T(8,128)(2,1)S(1)}, bf16[2,768,384]{1,2,0:T(8,128)(2,1)S(1)}, u32[]{:S(2)}, u32[]{:S(2)}) collective-permute-start(bf16[2,768,384]{1,2,0:T(8,128)(2,1)S(1)} %fusion.51), channel_id=1, source_target_pairs={{0,0},{1,16},{2,2},{3,18},{4,4},{5,20},{6,6},{7,22},{8,8},{9,24},{... | collective-permute-start | bytes 3538952 | tf_op jit(solution)/shard_map/ppermute | solution.py:84
  364.9 12.5 %collective-permute-start.16 = (bf16[2,768,384]{1,2,0:T(8,128)(2,1)S(1)}, bf16[2,768,384]{1,2,0:T(8,128)(2,1)S(1)}, u32[]{:S(2)}, u32[]{:S(2)}) collective-permute-start(bf16[2,768,384]{1,2,0:T(8,128)(2,1)S(1)} %add_convert_fusion.1), channel_id=1, source_target_pairs={{0,0},{1,16},{2,2},{3,18},{4,4},{5,20},{6,6},{7,22},{8,8},{9,24},{... | collective-permute-start | bytes 3538952 | tf_op jit(solution)/shard_map/ppermute | solution.py:84
  371.3 103.2 %collective-permute-start.14 = (bf16[512,768]{0,1:T(8,128)(2,1)}, bf16[512,768]{0,1:T(8,128)(2,1)S(1)}, u32[]{:S(2)}, u32[]{:S(2)}) collective-permute-start(bf16[512,768]{0,1:T(8,128)(2,1)} %fusion.61), channel_id=1, source_target_pairs={{0,0},{1,16},{2,2},{3,18},{4,4},{5,20},{6,6},{7,22},{8,8},{9,24},{... | collective-permute-start | bytes 2359304 | tf_op jit(solution)/shard_map/ppermute | solution.py:84
  377.4 22.0 %collective-permute-start.35 = (bf16[192,384]{0,1:T(8,128)(2,1)S(1)}, bf16[192,384]{0,1:T(8,128)(2,1)S(1)}, u32[]{:S(2)}, u32[]{:S(2)}) collective-permute-start(bf16[192,384]{0,1:T(8,128)(2,1)S(1)} %get-tuple-element.314), channel_id=1, source_target_pairs={{0,8},{4,12},{8,0},{12,4},{1,9},{5,13},{9,1},{13,5},{2,10},{6,14},... | collective-permute-start | bytes 442376 | tf_op jit(solution)/shard_map/ppermute | solution.py:118
  378.2 21.3 %collective-permute-start.17 = (bf16[768,384]{0,1:T(8,128)(2,1)S(1)}, bf16[768,384]{0,1:T(8,128)(2,1)S(1)}, u32[]{:S(2)}, u32[]{:S(2)}) collective-permute-start(bf16[768,384]{0,1:T(8,128)(2,1)S(1)} %dynamic-slice_bitcast_fusion.5), channel_id=1, source_target_pairs={{0,1},{1,0},{2,3},{3,2},{4,5},{5,4},{6,7},{7,6},{8,9},{9,8},{10,11... | collective-permute-start | bytes 1769480 | tf_op jit(solution)/shard_map/ppermute | solution.py:88
  385.6 14.5 %collective-permute-start.26 = (bf16[192,384]{0,1:T(8,128)(2,1)S(1)}, bf16[192,384]{0,1:T(8,128)(2,1)S(1)}, u32[]{:S(2)}, u32[]{:S(2)}) collective-permute-start(bf16[192,384]{0,1:T(8,128)(2,1)S(1)} %get-tuple-element.315), channel_id=1, source_target_pairs={{0,4},{4,8},{8,12},{12,0},{1,5},{5,9},{9,13},{13,1},{2,6},{6,10},{... | collective-permute-start | bytes 442376 | tf_op jit(solution)/shard_map/ppermute | solution.py:118
  387.2 19.2 %collective-permute-start.28 = (bf16[192,384]{0,1:T(8,128)(2,1)S(1)}, bf16[192,384]{0,1:T(8,128)(2,1)S(1)}, u32[]{:S(2)}, u32[]{:S(2)}) collective-permute-start(bf16[192,384]{0,1:T(8,128)(2,1)S(1)} %get-tuple-element.316), channel_id=1, source_target_pairs={{0,12},{4,0},{8,4},{12,8},{1,13},{5,1},{9,5},{13,9},{2,14},{6,2},{... | collective-permute-start | bytes 442376 | tf_op jit(solution)/shard_map/ppermute | solution.py:118
  399.4 16.9 %collective-permute-start.27 = (bf16[192,384]{0,1:T(8,128)(2,1)S(1)}, bf16[192,384]{0,1:T(8,128)(2,1)S(1)}, u32[]{:S(2)}, u32[]{:S(2)}) collective-permute-start(bf16[192,384]{0,1:T(8,128)(2,1)S(1)} %get-tuple-element.317), channel_id=1, source_target_pairs={{0,8},{4,12},{8,0},{12,4},{1,9},{5,13},{9,1},{13,5},{2,10},{6,14},... | collective-permute-start | bytes 442376 | tf_op jit(solution)/shard_map/ppermute | solution.py:118
  399.6 16.9 %collective-permute-start.37 = (bf16[1,192,384]{1,2,0:T(8,128)(2,1)S(1)}, bf16[1,192,384]{1,2,0:T(8,128)(2,1)S(1)}, u32[]{:S(2)}, u32[]{:S(2)}) collective-permute-start(bf16[1,192,384]{1,2,0:T(8,128)(2,1)S(1)} %fusion.86), channel_id=1, source_target_pairs={{0,1},{1,0},{2,3},{3,2},{4,5},{5,4},{6,7},{7,6},{8,9},{9,8},{10,11... | collective-permute-start | bytes 442376 | tf_op jit(solution)/shard_map/ppermute | solution.py:88
  400.2 16.5 %collective-permute-start.18 = (bf16[192,384]{0,1:T(8,128)(2,1)S(1)}, bf16[192,384]{0,1:T(8,128)(2,1)S(1)}, u32[]{:S(2)}, u32[]{:S(2)}) collective-permute-start(bf16[192,384]{0,1:T(8,128)(2,1)S(1)} %get-tuple-element.318), channel_id=1, source_target_pairs={{0,4},{4,8},{8,12},{12,0},{1,5},{5,9},{9,13},{13,1},{2,6},{6,10},{... | collective-permute-start | bytes 442376 | tf_op jit(solution)/shard_map/ppermute | solution.py:118
  406.5 13.9 %collective-permute-start.20 = (bf16[192,384]{0,1:T(8,128)(2,1)S(1)}, bf16[192,384]{0,1:T(8,128)(2,1)S(1)}, u32[]{:S(2)}, u32[]{:S(2)}) collective-permute-start(bf16[192,384]{0,1:T(8,128)(2,1)S(1)} %get-tuple-element.319), channel_id=1, source_target_pairs={{0,12},{4,0},{8,4},{12,8},{1,13},{5,1},{9,5},{13,9},{2,14},{6,2},{... | collective-permute-start | bytes 442376 | tf_op jit(solution)/shard_map/ppermute | solution.py:118
  416.3 12.5 %collective-permute-start.19 = (bf16[192,384]{0,1:T(8,128)(2,1)S(1)}, bf16[192,384]{0,1:T(8,128)(2,1)S(1)}, u32[]{:S(2)}, u32[]{:S(2)}) collective-permute-start(bf16[192,384]{0,1:T(8,128)(2,1)S(1)} %get-tuple-element.320), channel_id=1, source_target_pairs={{0,8},{4,12},{8,0},{12,4},{1,9},{5,13},{9,1},{13,5},{2,10},{6,14},... | collective-permute-start | bytes 442376 | tf_op jit(solution)/shard_map/ppermute | solution.py:118
  416.5 12.6 %collective-permute-start.29 = (bf16[1,192,384]{1,2,0:T(8,128)(2,1)S(1)}, bf16[1,192,384]{1,2,0:T(8,128)(2,1)S(1)}, u32[]{:S(2)}, u32[]{:S(2)}) collective-permute-start(bf16[1,192,384]{1,2,0:T(8,128)(2,1)S(1)} %fusion.85), channel_id=1, source_target_pairs={{0,1},{1,0},{2,3},{3,2},{4,5},{5,4},{6,7},{7,6},{8,9},{9,8},{10,11... | collective-permute-start | bytes 442376 | tf_op jit(solution)/shard_map/ppermute | solution.py:88
  416.7 61.4 %collective-permute-start.38 = (bf16[2,192,384]{1,2,0:T(8,128)(2,1)S(1)}, bf16[2,192,384]{1,2,0:T(8,128)(2,1)S(1)}, u32[]{:S(2)}, u32[]{:S(2)}) collective-permute-start(bf16[2,192,384]{1,2,0:T(8,128)(2,1)S(1)} %maximum_select_fusion.7), channel_id=1, source_target_pairs={{0,2},{1,3},{2,0},{3,1},{4,6},{5,7},{6,4},{7,5},{8,10},{9,11},{10,... | collective-permute-start | bytes 884744 | tf_op jit(solution)/shard_map/ppermute | solution.py:92
  429.0 46.6 %collective-permute-start.21 = (bf16[1,192,384]{1,2,0:T(8,128)(2,1)S(1)}, bf16[1,192,384]{1,2,0:T(8,128)(2,1)S(1)}, u32[]{:S(2)}, u32[]{:S(2)}) collective-permute-start(bf16[1,192,384]{1,2,0:T(8,128)(2,1)S(1)} %fusion.84), channel_id=1, source_target_pairs={{0,1},{1,0},{2,3},{3,2},{4,5},{5,4},{6,7},{7,6},{8,9},{9,8},{10,11... | collective-permute-start | bytes 442376 | tf_op jit(solution)/shard_map/ppermute | solution.py:88
  429.2 50.7 %collective-permute-start.30 = (bf16[2,192,384]{1,2,0:T(8,128)(2,1)S(1)}, bf16[2,192,384]{1,2,0:T(8,128)(2,1)}, u32[]{:S(2)}, u32[]{:S(2)}) collective-permute-start(bf16[2,192,384]{1,2,0:T(8,128)(2,1)S(1)} %maximum_select_fusion.6), channel_id=1, source_target_pairs={{0,2},{1,3},{2,0},{3,1},{4,6},{5,7},{6,4},{7,5},{8,10},{9,11},{10,... | collective-permute-start | bytes 884744 | tf_op jit(solution)/shard_map/ppermute | solution.py:92
  (56 other events, 651.8 us)
where the time goes:
time: 500 us; the launch traced here: 491 us
  matrix products  115 us (23%)
  starting transfers between devices  108 us (22%)
  local copies, waits for them, and re-layouts  85.6 us (17%)
  other arithmetic  76.4 us (15%)
  waiting for transfers between devices  52.5 us (10%)
  blocking collectives  42.3 us (8%)
  loops' own time  8.78 us (2%)
    ppermute x11, starting transfers between devices, swap_diagonal(): lax.ppermute(field, AXES, pairs_of(lambda t, d, r: (r % 2, d, r - r % 2 +...  68.4 us
    psum x1, blocking collectives, local(): lax.psum((grad_gain_one, grad_bias_one, grad_gain_two, grad_bias_two, dwa...  42.3 us
    dynamic_update_slice x4, local copies, waits for them, and re-layouts, local(): lax.scan(attend_back, (zero_heads, zero_heads), (block_starts, log_sums))  31.5 us
    ppermute x9, waiting for transfers between devices, reduce_pieces(): lax.ppermute(sent, 'dp', [(d, (d + step) % dps) for d in range(dps)])  30.4 us
    ppermute x6, waiting for transfers between devices, swap_far(): lax.ppermute(field, 'rep', [(r, r ^ 2) for r in range(lax.axis_size('rep'...  20.4 us
    unnamed x98, local copies, waits for them, and re-layouts  20.3 us
    dot_general x2, matrix products, attend_back(): jnp.einsum('qhe,khe->hqk', grad_block_rows, values, preferred_element_typ...  17 us
    ppermute x13, starting transfers between devices, swap_near(): lax.ppermute(field, 'rep', [(r, r ^ 1) for r in range(lax.axis_size('rep'...  15.7 us
  transfers between devices with their start and end apart: 39, of which 7 were waited for; matrix products, arithmetic and copies ran while one was open for 53% of the time, Pallas kernels for 0%

commit v1 on v0

--- a/solution.py
+++ b/solution.py
@@ -315,7 +315,10 @@
     grad_resid_half = lax.dynamic_slice_in_dim(grad_resid, near * rows, rows, 0)
     grad_input = swap_diagonal((grad_resid_half + grad_rows_norm).astype(jnp.bfloat16))
     small_sums = lax.psum(
-        (grad_gain_one, grad_bias_one, grad_gain_two, grad_bias_two, dwa_terms), AXES
+        lax.psum(
+            (grad_gain_one, grad_bias_one, grad_gain_two, grad_bias_two, dwa_terms), ("dp", "rep")
+        ),
+        "tp",
     )
     return (
         output.astype(jnp.bfloat16)[None],

time: 500 us -> 521 us (1.042)
  blocking collectives: 42.3 us -> 66.6 us
    psum x1, blocking collectives: 42.3 us -> 59 us  [local(): lax.psum((grad_gain_one, grad_bias_one, grad_gain_two, grad_bias_two, dwa...]
    psum x0 -> x1, blocking collectives: none -> 7.59 us  [local(): lax.psum(lax.psum((grad_gain_one, grad_bias_one, grad_gain_two, grad_bias...]
  transfers between devices with their start and end apart: 39 -> 39, of which waited for: 7 -> 7; matrix products, arithmetic and copies ran while one was open for 53% -> 51% of each run, Pallas kernels for 0% -> 0%
where the time goes in v1:
time: 521 us; the launch traced here: 512 us
  matrix products  115 us (22%)
  starting transfers between devices  105 us (20%)
  local copies, waits for them, and re-layouts  85.5 us (16%)
  other arithmetic  76.2 us (15%)
  blocking collectives  66.6 us (13%)
  waiting for transfers between devices  52.1 us (10%)
  loops' own time  8.47 us (2%)
    ppermute x11, starting transfers between devices, swap_diagonal(): lax.ppermute(field, AXES, pairs_of(lambda t, d, r: (r % 2, d, r - r % 2 +...  68.4 us
    psum x1, blocking collectives, local(): lax.psum((grad_gain_one, grad_bias_one, grad_gain_two, grad_bias_two, dwa...  59 us
    dynamic_update_slice x4, local copies, waits for them, and re-layouts, local(): lax.scan(attend_back, (zero_heads, zero_heads), (block_starts, log_sums))  31.5 us
    ppermute x9, waiting for transfers between devices, reduce_pieces(): lax.ppermute(sent, 'dp', [(d, (d + step) % dps) for d in range(dps)])  30.4 us
    unnamed x98, local copies, waits for them, and re-layouts  20.3 us
    ppermute x6, waiting for transfers between devices, swap_far(): lax.ppermute(field, 'rep', [(r, r ^ 2) for r in range(lax.axis_size('rep'...  20 us
    dot_general x2, matrix products, attend_back(): jnp.einsum('qhe,khe->hqk', grad_block_rows, values, preferred_element_typ...  17 us
    ppermute x13, starting transfers between devices, swap_near(): lax.ppermute(field, 'rep', [(r, r ^ 1) for r in range(lax.axis_size('rep'...  15.6 us
  transfers between devices with their start and end apart: 39, of which 7 were waited for; matrix products, arithmetic and copies ran while one was open for 51% of the time, Pallas kernels for 0%

profile of v1, /device:TPU:0, one launch (start us, length us, event | category | flops | bytes accessed | tf_op | source)
XLA Modules:
  0.0 511.5 jit_solution(860059539975653087)
XLA Ops:
  8.1 6.0 %collective-permute-start.4 = (bf16[384,768]{1,0:T(8,128)(2,1)}, bf16[384,768]{1,0:T(8,128)(2,1)}, u32[]{:S(2)}, u32[]{:S(2)}) collective-permute-start(bf16[384,768]{1,0:T(8,128)(2,1)} %param.25), channel_id=1, source_target_pairs={{0,0},{1,16},{2,2},{3,18},{4,4},{5,20},{6,6},{7,22},{8,8},{9,24},{... | collective-permute-start | bytes 1769480 | tf_op jit(solution)/shard_map/ppermute | solution.py:84
  16.4 7.6 %collective-permute-start.10 = (bf16[512,768]{0,1:T(8,128)(2,1)}, bf16[512,768]{0,1:T(8,128)(2,1)}, u32[]{:S(2)}, u32[]{:S(2)}) collective-permute-start(bf16[512,768]{0,1:T(8,128)(2,1)} %bitcast.14), channel_id=1, source_target_pairs={{0,0},{1,16},{2,2},{3,18},{4,4},{5,20},{6,6},{7,22},{8,8},{9,24},{... | collective-permute-start | bytes 2359304 | tf_op jit(solution)/shard_map/ppermute | solution.py:84
  28.4 19.3 %collective-permute-start.6 = (bf16[768,1536]{1,0:T(8,128)(2,1)}, bf16[768,1536]{1,0:T(8,128)(2,1)}, u32[]{:S(2)}, u32[]{:S(2)}) collective-permute-start(bf16[768,1536]{1,0:T(8,128)(2,1)} %param.28), channel_id=1, source_target_pairs={{0,0},{1,16},{2,2},{3,18},{4,4},{5,20},{6,6},{7,22},{8,8},{9,24},{... | collective-permute-start | bytes 7077896 | tf_op jit(solution)/shard_map/ppermute | solution.py:84
  50.3 19.7 %collective-permute-start.7 = (bf16[1536,768]{1,0:T(8,128)(2,1)}, bf16[1536,768]{1,0:T(8,128)(2,1)}, u32[]{:S(2)}, u32[]{:S(2)}) collective-permute-start(bf16[1536,768]{1,0:T(8,128)(2,1)} %param.29), channel_id=1, source_target_pairs={{0,0},{1,16},{2,2},{3,18},{4,4},{5,20},{6,6},{7,22},{8,8},{9,24},{... | collective-permute-start | bytes 7077896 | tf_op jit(solution)/shard_map/ppermute | solution.py:84
  76.4 35.6 %while.28 = (s32[]{:T(128)}, bf16[2,512,384]{2,1,0:T(8,128)(2,1)}, f32[2,6,512]{2,1,0:T(8,128)S(1)}, s32[2]{0:T(128)S(1)}, s32[1024]{0:T(1024)S(1)}, /*index=5*/...) while((s32[]{:T(128)}, bf16[2,512,384]{2,1,0:T(8,128)(2,1)}, ...), condition=%wide.region_9.10_spmd.clone, body=%wide.region_6.9_spmd.clone.sunk | while | flops 844822016 | bytes 50194668 | solution.py:197
  87.8 5.1 fusion.140
  105.5 5.1 fusion.140
  119.8 5.2 %fusion.35 = (f32[4]{0:T(128)}, f32[512,768]{1,0:T(8,128)}) fusion(bf16[4,1,512,768]{3,2,1,0:T(8,128)(2,1)} %param.18, f32[512,768]{1,0:T(8,128)S(1)} %copy.124, f32[4]{0:T(128)S(1)} %bitcast.181), kind=kLoop, calls=%fused_computation.50 | loop fusion | flops 7471100 | bytes 6291488 | tf_op jit(solution)/shard_map/reduce_sum | solution.py:240
  137.8 5.8 %fusion.91 = f32[1024,1536]{1,0:T(8,128)S(1)} fusion(bf16[768,1536]{1,0:T(8,128)(2,1)} %collective-permute-done.6, f32[1024,768]{0,1:T(8,128)S(1)} %subtract_multiply_fusion, f32[768]{0:T(1024)S(1)} %copy-done.41, f32[768]{0:T(1024)S(1)} %copy-done.30), kind=kOutput, calls=%fused_computation.206 | convolution fusion | flops 2418278400 | bytes 11802624 | tf_op jit(solution)/shard_map/dot_general | solution.py:203
  146.5 6.9 %convolution_convert_fusion = bf16[768,1536]{1,0:T(8,128)(2,1)} fusion(f32[]{:T(128)} %bitcast.1, bf16[512,768]{0,1:T(8,128)(2,1)S(1)} %collective-permute-done.11, bf16[512,768]{0,1:T(8,128)(2,1)} %collective-permute-done.10, pred[]{:T(512)S(6)} %eq.64, f32[1024,1536]{1,0:T(8,128)S(1)} %fusion.91), kind=kOutput, calls=%fused_computation.65 | convolution fusion | flops 2440691712 | bytes 10223621 | tf_op jit(solution)/shard_map/td,tf->df/dot_general | solution.py:215
  161.8 10.7 %fusion.42 = bf16[1024,1536]{1,0:T(8,128)(2,1)S(1)} fusion(f32[1024,1536]{1,0:T(8,128)} %copy-done.44, bf16[1536,768]{1,0:T(8,128)(2,1)} %collective-permute-done.7, f32[]{:T(128)} %bitcast.1, bf16[512,768]{0,1:T(8,128)(2,1)S(1)} %copy-done.25, bf16[512,768]{0,1:T(8,128)(2,1)} %collective-permute-done.10, pred[]{:T(512)S(6)} %eq.64), kind=kOutput, calls=%fused_computation.57 | convolution fusion | flops 2456813568 | bytes 13369349 | tf_op jit(solution)/shard_map/td,fd->tf/dot_general | solution.py:208
  172.5 5.5 %convolution_convert_fusion.3 = bf16[1024,768]{0,1:T(8,128)(2,1)} fusion(bf16[1024,1536]{1,0:T(8,128)(2,1)S(1)} %fusion.42, bf16[768,1536]{1,0:T(8,128)(2,1)} %collective-permute-done.6), kind=kOutput, calls=%fused_computation.103 | convolution fusion | flops 2416705536 | bytes 7077888 | tf_op jit(solution)/shard_map/tf,df->td/dot_general | solution.py:211
  178.0 5.0 fusion.92
  200.9 7.6 %collective-permute-start.9 = (bf16[512,768]{0,1:T(8,128)(2,1)}, bf16[512,768]{0,1:T(8,128)(2,1)}, u32[]{:S(2)}, u32[]{:S(2)}) collective-permute-start(bf16[512,768]{0,1:T(8,128)(2,1)} %add_convert_fusion.2), channel_id=1, source_target_pairs={{0,0},{1,16},{2,2},{3,18},{4,4},{5,20},{6,6},{7,22},{8,8},{9,24},{... | collective-permute-start | bytes 2359304 | tf_op jit(solution)/shard_map/ppermute | solution.py:84
  213.1 4.9 multiply_add_fusion
  222.5 96.8 %while.29 = (s32[]{:T(128)}, f32[1024,6,64]{0,2,1:T(8,128)S(1)}, f32[1024,6,64]{0,2,1:T(8,128)}, f32[2,512,6,64]{1,0,3,2:T(2,128)}, s32[2]{0:T(128)S(1)}, /*inde...) while((s32[]{:T(128)}, f32[1024,6,64]{0,2,1:T(8,128)S(1)}, ...), condition=%wide.region_18.19_spmd.clone, body=%wide.region_16.18_spmd.clone.sunk | while | flops 2064184832 | bytes 110725352 | solution.py:292
  229.4 5.6 %bitcast_add_fusion.7 = f32[1024,6,64]{0,2,1:T(8,128)} fusion(f32[1024,6,64]{0,2,1:T(8,128)} %get-tuple-element.507, f32[6,512,1024]{2,1,0:T(8,128)S(1)} %fusion.150, f32[6,512]{1,0:T(8,128)S(1)} %dynamic-slice_bitcast_fusion.7, pred[512,1024]{1,0:T(8,128)(4,1)S(1)} %fusion.151, pred[]{:T(512)S(6)} %compare.9, ...), kind=kOutput, calls=%fused_computation.27.clone.1 | convolution fusion | flops 416022528 | bytes 16658437 | tf_op jit(solution)/shard_map/while/body/eval_jaxpr/hqk,qhe->khe/dot_general | solution.py:275
  235.0 8.5 %multiply_reduce_fusion.7 = (f32[6,512]{1,0:T(8,128)S(1)}, f32[6,512,1024]{2,1,0:T(8,128)}) fusion(f32[6,512,1024]{2,1,0:T(8,128)S(1)} %fusion.150, f32[6,512]{1,0:T(8,128)S(1)} %dynamic-slice_bitcast_fusion.7, pred[512,1024]{1,0:T(8,128)(4,1)S(1)} %fusion.151, bf16[1024,6,64]{0,2,1:T(8,128)(2,1)} %get-tuple-element.529, ...), kind=kOutput, calls=%fused_computation.20.clone.1 | convolution fusion | flops 418378752 | bytes 26894340 | tf_op jit(solution)/shard_map/while/body/eval_jaxpr/qhe,khe->hqk/dot_general | solution.py:278
  243.5 6.9 %multiply_convert_fusion.6 = bf16[6,512,1024]{2,1,0:T(8,128)(2,1)S(1)} fusion(f32[6,512,1024]{2,1,0:T(8,128)} %get-tuple-element.456, f32[6,512,1024]{2,1,0:T(8,128)S(1)} %fusion.150, f32[6,512]{1,0:T(8,128)S(1)} %get-tuple-element.457, f32[6,512]{1,0:T(8,128)S(1)} %dynamic-slice_bitcast_fusion.7, pred[512,1024]{1,0:T(8,128)(4,1)S(1)} %fusion.151), kind=kLoop, calls=%fused_computation.19.clone.1 | loop fusion | flops 18874368 | bytes 32006144 | tf_op jit(solution)/shard_map/while/body/eval_jaxpr/convert_element_type | solution.py:282
  255.7 14.9 %dynamic_update_slice.22 = f32[2,512,6,64]{1,0,3,2:T(2,128)} dynamic-update-slice(f32[2,512,6,64]{1,0,3,2:T(2,128)} %get-tuple-element.508, f32[1,512,6,64]{1,0,3,2:T(1,128)S(1)} %copy.173, s32[]{:T(128)S(6)} %copy.190, s32[]{:T(128)} %constant.132.clone.1..sunk.1, s32[]{:T(128)} %constant.132.clone.1..sunk.1, s32[]{:T(128)} %constant.132.clone.1..sunk.1) | dynamic-update-slice | bytes 1572868 | tf_op jit(solution)/shard_map/while/body/jit(dynamic_update_index_in_dim)/dynamic_update_slice | solution.py:292
  277.4 6.1 %bitcast_add_fusion.7 = f32[1024,6,64]{0,2,1:T(8,128)} fusion(f32[1024,6,64]{0,2,1:T(8,128)} %get-tuple-element.507, f32[6,512,1024]{2,1,0:T(8,128)S(1)} %fusion.150, f32[6,512]{1,0:T(8,128)S(1)} %dynamic-slice_bitcast_fusion.7, pred[512,1024]{1,0:T(8,128)(4,1)S(1)} %fusion.151, pred[]{:T(512)S(6)} %compare.9, ...), kind=kOutput, calls=%fused_computation.27.clone.1 | convolution fusion | flops 416022528 | bytes 16658437 | tf_op jit(solution)/shard_map/while/body/eval_jaxpr/hqk,qhe->khe/dot_general | solution.py:275
  283.5 8.5 %multiply_reduce_fusion.7 = (f32[6,512]{1,0:T(8,128)S(1)}, f32[6,512,1024]{2,1,0:T(8,128)}) fusion(f32[6,512,1024]{2,1,0:T(8,128)S(1)} %fusion.150, f32[6,512]{1,0:T(8,128)S(1)} %dynamic-slice_bitcast_fusion.7, pred[512,1024]{1,0:T(8,128)(4,1)S(1)} %fusion.151, bf16[1024,6,64]{0,2,1:T(8,128)(2,1)} %get-tuple-element.529, ...), kind=kOutput, calls=%fused_computation.20.clone.1 | convolution fusion | flops 418378752 | bytes 26894340 | tf_op jit(solution)/shard_map/while/body/eval_jaxpr/qhe,khe->hqk/dot_general | solution.py:278
  292.0 6.9 %multiply_convert_fusion.6 = bf16[6,512,1024]{2,1,0:T(8,128)(2,1)S(1)} fusion(f32[6,512,1024]{2,1,0:T(8,128)} %get-tuple-element.456, f32[6,512,1024]{2,1,0:T(8,128)S(1)} %fusion.150, f32[6,512]{1,0:T(8,128)S(1)} %get-tuple-element.457, f32[6,512]{1,0:T(8,128)S(1)} %dynamic-slice_bitcast_fusion.7, pred[512,1024]{1,0:T(8,128)(4,1)S(1)} %fusion.151), kind=kLoop, calls=%fused_computation.19.clone.1 | loop fusion | flops 18874368 | bytes 32006144 | tf_op jit(solution)/shard_map/while/body/eval_jaxpr/convert_element_type | solution.py:282
  304.2 14.9 %dynamic_update_slice.22 = f32[2,512,6,64]{1,0,3,2:T(2,128)} dynamic-update-slice(f32[2,512,6,64]{1,0,3,2:T(2,128)} %get-tuple-element.508, f32[1,512,6,64]{1,0,3,2:T(1,128)S(1)} %copy.173, s32[]{:T(128)S(6)} %copy.190, s32[]{:T(128)} %constant.132.clone.1..sunk.1, s32[]{:T(128)} %constant.132.clone.1..sunk.1, s32[]{:T(128)} %constant.132.clone.1..sunk.1) | dynamic-update-slice | bytes 1572868 | tf_op jit(solution)/shard_map/while/body/jit(dynamic_update_index_in_dim)/dynamic_update_slice | solution.py:292
  346.9 16.9 %collective-permute-done.15 = bf16[2,768,384]{1,2,0:T(8,128)(2,1)S(1)} collective-permute-done((bf16[2,768,384]{1,2,0:T(8,128)(2,1)S(1)}, bf16[2,768,384]{1,2,0:T(8,128)(2,1)S(1)}, u32[]{:S(2)}, u32[]{:S(2)}) %collective-permute-start.15) | collective-permute-done | bytes 1179680 | tf_op jit(solution)/shard_map/ppermute | solution.py:92
  377.6 6.9 %collective-permute-start.17 = (bf16[768,384]{0,1:T(8,128)(2,1)S(1)}, bf16[768,384]{0,1:T(8,128)(2,1)S(1)}, u32[]{:S(2)}, u32[]{:S(2)}) collective-permute-start(bf16[768,384]{0,1:T(8,128)(2,1)S(1)} %dynamic-slice_bitcast_fusion.5), channel_id=1, source_target_pairs={{0,1},{1,0},{2,3},{3,2},{4,5},{5,4},{6,7},{7,6},{8,9},{9,8},{10,11... | collective-permute-start | bytes 1769480 | tf_op jit(solution)/shard_map/ppermute | solution.py:88
  388.9 9.9 %collective-permute-done.35 = bf16[192,384]{0,1:T(8,128)(2,1)S(1)} collective-permute-done((bf16[192,384]{0,1:T(8,128)(2,1)S(1)}, bf16[192,384]{0,1:T(8,128)(2,1)S(1)}, u32[]{:S(2)}, u32[]{:S(2)}) %collective-permute-start.35) | collective-permute-done | bytes 147488 | tf_op jit(solution)/shard_map/ppermute | solution.py:118
  399.6 6.3 %collective-permute-start.18 = (bf16[192,384]{0,1:T(8,128)(2,1)S(1)}, bf16[192,384]{0,1:T(8,128)(2,1)S(1)}, u32[]{:S(2)}, u32[]{:S(2)}) collective-permute-start(bf16[192,384]{0,1:T(8,128)(2,1)S(1)} %get-tuple-element.323), channel_id=1, source_target_pairs={{0,4},{4,8},{8,12},{12,0},{1,5},{5,9},{9,13},{13,1},{2,6},{6,10},{... | collective-permute-start | bytes 442376 | tf_op jit(solution)/shard_map/ppermute | solution.py:118
  405.8 9.8 %collective-permute-done.27 = bf16[192,384]{0,1:T(8,128)(2,1)S(1)} collective-permute-done((bf16[192,384]{0,1:T(8,128)(2,1)S(1)}, bf16[192,384]{0,1:T(8,128)(2,1)S(1)}, u32[]{:S(2)}, u32[]{:S(2)}) %collective-permute-start.27) | collective-permute-done | bytes 147488 | tf_op jit(solution)/shard_map/ppermute | solution.py:118
  419.8 8.5 %collective-permute-done.19 = bf16[192,384]{0,1:T(8,128)(2,1)S(1)} collective-permute-done((bf16[192,384]{0,1:T(8,128)(2,1)S(1)}, bf16[192,384]{0,1:T(8,128)(2,1)S(1)}, u32[]{:S(2)}, u32[]{:S(2)}) %collective-permute-start.19) | collective-permute-done | bytes 147488 | tf_op jit(solution)/shard_map/ppermute | solution.py:118
  431.6 59.0 %all-reduce = (f32[5]{0:T(128)S(1)}, f32[768]{0:T(1024)S(1)}, f32[768]{0:T(1024)S(1)}, f32[768]{0:T(1024)S(1)}, f32[768]{0:T(1024)S(1)}) all-reduce(f32[5]{0:T(128)S(1)} %pad_maximum_fusion.7, f32[768]{0:T(1024)S(1)} %get-tuple-element.239, f32[768]{0:T(1024)S(1)} %get-tuple-element.242, ...), channel_id=1, replica_groups=mesh['tp'=2,'dp'=4,'rep'=4] {'dp','rep'}, use_global_device_ids=true, to_apply=%region_23.24 | all-reduce | flops 3077 | bytes 24616 | tf_op jit(solution)/shard_map/psum | solution.py:318
  490.6 7.6 %all-reduce.1 = (f32[5]{0:T(128)}, f32[768]{0:T(1024)}, f32[768]{0:T(1024)}, f32[768]{0:T(1024)}, f32[768]{0:T(1024)}) all-reduce(f32[5]{0:T(128)S(1)} %get-tuple-element.281, f32[768]{0:T(1024)S(1)} %get-tuple-element.282, f32[768]{0:T(1024)S(1)} %get-tuple-element.283, ...), channel_id=1, replica_groups=mesh['tp'=2,'dp'=4,'rep'=4] {'tp'}, use_global_device_ids=true, to_apply=%region_24.25 | all-reduce | flops 3077 | bytes 24616 | tf_op jit(solution)/shard_map/psum | solution.py:317
  (303 shorter events, 189.6 us)
Async XLA Ops:
  3.1 44.9 %collective-permute-start = (bf16[512,768]{0,1:T(8,128)(2,1)}, bf16[512,768]{0,1:T(8,128)(2,1)S(1)}, u32[]{:S(2)}, u32[]{:S(2)}) collective-permute-start(bf16[512,768]{0,1:T(8,128)(2,1)} %bitcast.177), channel_id=1, source_target_pairs={{0,0},{1,16},{2,2},{3,18},{4,4},{5,20},{6,6},{7,22},{8,8},{9,24},{... | collective-permute-start | bytes 2359304 | tf_op jit(solution)/shard_map/ppermute | solution.py:84
  4.9 23.5 %collective-permute-start.2 = (s32[1,3]{1,0:T(1,128)}, s32[1,3]{1,0:T(1,128)S(1)}, u32[]{:S(2)}, u32[]{:S(2)}) collective-permute-start(s32[1,3]{1,0:T(1,128)} %param.20), channel_id=1, source_target_pairs={{0,1},{1,0},{2,3},{3,2},{4,5},{5,4},{6,7},{7,6},{8,9},{9,8},{10,11... | collective-permute-start | bytes 44 | tf_op jit(solution)/shard_map/ppermute | solution.py:88
  8.1 103.8 %collective-permute-start.4 = (bf16[384,768]{1,0:T(8,128)(2,1)}, bf16[384,768]{1,0:T(8,128)(2,1)}, u32[]{:S(2)}, u32[]{:S(2)}) collective-permute-start(bf16[384,768]{1,0:T(8,128)(2,1)} %param.25), channel_id=1, source_target_pairs={{0,0},{1,16},{2,2},{3,18},{4,4},{5,20},{6,6},{7,22},{8,8},{9,24},{... | collective-permute-start | bytes 1769480 | tf_op jit(solution)/shard_map/ppermute | solution.py:84
  16.4 114.7 %collective-permute-start.10 = (bf16[512,768]{0,1:T(8,128)(2,1)}, bf16[512,768]{0,1:T(8,128)(2,1)}, u32[]{:S(2)}, u32[]{:S(2)}) collective-permute-start(bf16[512,768]{0,1:T(8,128)(2,1)} %bitcast.14), channel_id=1, source_target_pairs={{0,0},{1,16},{2,2},{3,18},{4,4},{5,20},{6,6},{7,22},{8,8},{9,24},{... | collective-permute-start | bytes 2359304 | tf_op jit(solution)/shard_map/ppermute | solution.py:84
  26.2 45.0 %collective-permute-start.3 = (bf16[3,768,384]{1,2,0:T(8,128)(2,1)}, bf16[3,768,384]{1,2,0:T(8,128)(2,1)S(1)}, u32[]{:S(2)}, u32[]{:S(2)}) collective-permute-start(bf16[3,768,384]{1,2,0:T(8,128)(2,1)} %copy.109), channel_id=1, source_target_pairs={{0,0},{1,16},{2,2},{3,18},{4,4},{5,20},{6,6},{7,22},{8,8},{9,24},{... | collective-permute-start | bytes 5308424 | tf_op jit(solution)/shard_map/ppermute | solution.py:84
  28.4 109.4 %collective-permute-start.6 = (bf16[768,1536]{1,0:T(8,128)(2,1)}, bf16[768,1536]{1,0:T(8,128)(2,1)}, u32[]{:S(2)}, u32[]{:S(2)}) collective-permute-start(bf16[768,1536]{1,0:T(8,128)(2,1)} %param.28), channel_id=1, source_target_pairs={{0,0},{1,16},{2,2},{3,18},{4,4},{5,20},{6,6},{7,22},{8,8},{9,24},{... | collective-permute-start | bytes 7077896 | tf_op jit(solution)/shard_map/ppermute | solution.py:84
  50.3 111.5 %collective-permute-start.7 = (bf16[1536,768]{1,0:T(8,128)(2,1)}, bf16[1536,768]{1,0:T(8,128)(2,1)}, u32[]{:S(2)}, u32[]{:S(2)}) collective-permute-start(bf16[1536,768]{1,0:T(8,128)(2,1)} %param.29), channel_id=1, source_target_pairs={{0,0},{1,16},{2,2},{3,18},{4,4},{5,20},{6,6},{7,22},{8,8},{9,24},{... | collective-permute-start | bytes 7077896 | tf_op jit(solution)/shard_map/ppermute | solution.py:84
  115.4 17.2 %collective-permute-start.5 = (bf16[1024,768]{0,1:T(8,128)(2,1)}, bf16[1024,768]{0,1:T(8,128)(2,1)}, u32[]{:S(2)}, u32[]{:S(2)}) collective-permute-start(bf16[1024,768]{0,1:T(8,128)(2,1)} %convolution_convert_fusion.2), channel_id=1, source_target_pairs={{0,1},{1,0},{2,3},{3,2},{4,5},{5,4},{6,7},{7,6},{8,9},{9,8},{10,11... | collective-permute-start | bytes 4718600 | tf_op jit(solution)/shard_map/ppermute | solution.py:88
  131.1 12.5 %collective-permute-start.11 = (bf16[512,768]{0,1:T(8,128)(2,1)}, bf16[512,768]{0,1:T(8,128)(2,1)S(1)}, u32[]{:S(2)}, u32[]{:S(2)}) collective-permute-start(bf16[512,768]{0,1:T(8,128)(2,1)} %collective-permute-done.10), channel_id=1, source_target_pairs={{0,1},{1,0},{2,3},{3,2},{4,5},{5,4},{6,7},{7,6},{8,9},{9,8},{10,11... | collective-permute-start | bytes 2359304 | tf_op jit(solution)/shard_map/ppermute | solution.py:88
  160.3 176.8 %collective-permute-start.31 = (bf16[2,768,384]{1,2,0:T(8,128)(2,1)}, bf16[2,768,384]{1,2,0:T(8,128)(2,1)}, u32[]{:S(2)}, u32[]{:S(2)}) collective-permute-start(bf16[2,768,384]{1,2,0:T(8,128)(2,1)} %dynamic-slice_bitcast_fusion.1), channel_id=1, source_target_pairs={{0,2},{1,3},{2,0},{3,1},{4,6},{5,7},{6,4},{7,5},{8,10},{9,11},{10,... | collective-permute-start | bytes 3538952 | tf_op jit(solution)/shard_map/ppermute | solution.py:92
  178.0 30.6 %collective-permute-start.12 = (bf16[1024,768]{0,1:T(8,128)(2,1)}, bf16[1024,768]{0,1:T(8,128)(2,1)}, u32[]{:S(2)}, u32[]{:S(2)}) collective-permute-start(bf16[1024,768]{0,1:T(8,128)(2,1)} %convolution_convert_fusion.3), channel_id=1, source_target_pairs={{0,1},{1,0},{2,3},{3,2},{4,5},{5,4},{6,7},{7,6},{8,9},{9,8},{10,11... | collective-permute-start | bytes 4718600 | tf_op jit(solution)/shard_map/ppermute | solution.py:88
  197.0 142.5 %collective-permute-start.23 = (bf16[2,768,384]{1,2,0:T(8,128)(2,1)}, bf16[2,768,384]{1,2,0:T(8,128)(2,1)}, u32[]{:S(2)}, u32[]{:S(2)}) collective-permute-start(bf16[2,768,384]{1,2,0:T(8,128)(2,1)} %dynamic-slice_bitcast_fusion.2), channel_id=1, source_target_pairs={{0,2},{1,3},{2,0},{3,1},{4,6},{5,7},{6,4},{7,5},{8,10},{9,11},{10,... | collective-permute-start | bytes 3538952 | tf_op jit(solution)/shard_map/ppermute | solution.py:92
  200.9 141.2 %collective-permute-start.9 = (bf16[512,768]{0,1:T(8,128)(2,1)}, bf16[512,768]{0,1:T(8,128)(2,1)}, u32[]{:S(2)}, u32[]{:S(2)}) collective-permute-start(bf16[512,768]{0,1:T(8,128)(2,1)} %add_convert_fusion.2), channel_id=1, source_target_pairs={{0,0},{1,16},{2,2},{3,18},{4,4},{5,20},{6,6},{7,22},{8,8},{9,24},{... | collective-permute-start | bytes 2359304 | tf_op jit(solution)/shard_map/ppermute | solution.py:84
  332.4 13.6 %collective-permute-start.13 = (bf16[512,768]{0,1:T(8,128)(2,1)S(1)}, bf16[512,768]{0,1:T(8,128)(2,1)S(1)}, u32[]{:S(2)}, u32[]{:S(2)}) collective-permute-start(bf16[512,768]{0,1:T(8,128)(2,1)S(1)} %dynamic-slice_convert_fusion), channel_id=1, source_target_pairs={{0,1},{1,0},{2,3},{3,2},{4,5},{5,4},{6,7},{7,6},{8,9},{9,8},{10,11... | collective-permute-start | bytes 2359304 | tf_op jit(solution)/shard_map/ppermute | solution.py:88
  335.6 28.2 %collective-permute-start.15 = (bf16[2,768,384]{1,2,0:T(8,128)(2,1)S(1)}, bf16[2,768,384]{1,2,0:T(8,128)(2,1)S(1)}, u32[]{:S(2)}, u32[]{:S(2)}) collective-permute-start(bf16[2,768,384]{1,2,0:T(8,128)(2,1)S(1)} %fusion.74), channel_id=1, source_target_pairs={{0,2},{1,3},{2,0},{3,1},{4,6},{5,7},{6,4},{7,5},{8,10},{9,11},{10,... | collective-permute-start | bytes 3538952 | tf_op jit(solution)/shard_map/ppermute | solution.py:92
  338.7 26.4 %collective-permute-start.32 = (bf16[2,768,384]{1,2,0:T(8,128)(2,1)S(1)}, bf16[2,768,384]{1,2,0:T(8,128)(2,1)S(1)}, u32[]{:S(2)}, u32[]{:S(2)}) collective-permute-start(bf16[2,768,384]{1,2,0:T(8,128)(2,1)S(1)} %fusion.50), channel_id=1, source_target_pairs={{0,0},{1,16},{2,2},{3,18},{4,4},{5,20},{6,6},{7,22},{8,8},{9,24},{... | collective-permute-start | bytes 3538952 | tf_op jit(solution)/shard_map/ppermute | solution.py:84
  341.2 24.9 %collective-permute-start.24 = (bf16[2,768,384]{1,2,0:T(8,128)(2,1)S(1)}, bf16[2,768,384]{1,2,0:T(8,128)(2,1)S(1)}, u32[]{:S(2)}, u32[]{:S(2)}) collective-permute-start(bf16[2,768,384]{1,2,0:T(8,128)(2,1)S(1)} %fusion.51), channel_id=1, source_target_pairs={{0,0},{1,16},{2,2},{3,18},{4,4},{5,20},{6,6},{7,22},{8,8},{9,24},{... | collective-permute-start | bytes 3538952 | tf_op jit(solution)/shard_map/ppermute | solution.py:84
  364.4 12.5 %collective-permute-start.16 = (bf16[2,768,384]{1,2,0:T(8,128)(2,1)S(1)}, bf16[2,768,384]{1,2,0:T(8,128)(2,1)S(1)}, u32[]{:S(2)}, u32[]{:S(2)}) collective-permute-start(bf16[2,768,384]{1,2,0:T(8,128)(2,1)S(1)} %add_convert_fusion.1), channel_id=1, source_target_pairs={{0,0},{1,16},{2,2},{3,18},{4,4},{5,20},{6,6},{7,22},{8,8},{9,24},{... | collective-permute-start | bytes 3538952 | tf_op jit(solution)/shard_map/ppermute | solution.py:84
  370.7 127.5 %collective-permute-start.14 = (bf16[512,768]{0,1:T(8,128)(2,1)}, bf16[512,768]{0,1:T(8,128)(2,1)S(1)}, u32[]{:S(2)}, u32[]{:S(2)}) collective-permute-start(bf16[512,768]{0,1:T(8,128)(2,1)} %fusion.61), channel_id=1, source_target_pairs={{0,0},{1,16},{2,2},{3,18},{4,4},{5,20},{6,6},{7,22},{8,8},{9,24},{... | collective-permute-start | bytes 2359304 | tf_op jit(solution)/shard_map/ppermute | solution.py:84
  376.8 22.0 %collective-permute-start.35 = (bf16[192,384]{0,1:T(8,128)(2,1)S(1)}, bf16[192,384]{0,1:T(8,128)(2,1)S(1)}, u32[]{:S(2)}, u32[]{:S(2)}) collective-permute-start(bf16[192,384]{0,1:T(8,128)(2,1)S(1)} %get-tuple-element.319), channel_id=1, source_target_pairs={{0,8},{4,12},{8,0},{12,4},{1,9},{5,13},{9,1},{13,5},{2,10},{6,14},... | collective-permute-start | bytes 442376 | tf_op jit(solution)/shard_map/ppermute | solution.py:118
  377.6 21.4 %collective-permute-start.17 = (bf16[768,384]{0,1:T(8,128)(2,1)S(1)}, bf16[768,384]{0,1:T(8,128)(2,1)S(1)}, u32[]{:S(2)}, u32[]{:S(2)}) collective-permute-start(bf16[768,384]{0,1:T(8,128)(2,1)S(1)} %dynamic-slice_bitcast_fusion.5), channel_id=1, source_target_pairs={{0,1},{1,0},{2,3},{3,2},{4,5},{5,4},{6,7},{7,6},{8,9},{9,8},{10,11... | collective-permute-start | bytes 1769480 | tf_op jit(solution)/shard_map/ppermute | solution.py:88
  385.0 14.5 %collective-permute-start.26 = (bf16[192,384]{0,1:T(8,128)(2,1)S(1)}, bf16[192,384]{0,1:T(8,128)(2,1)S(1)}, u32[]{:S(2)}, u32[]{:S(2)}) collective-permute-start(bf16[192,384]{0,1:T(8,128)(2,1)S(1)} %get-tuple-element.320), channel_id=1, source_target_pairs={{0,4},{4,8},{8,12},{12,0},{1,5},{5,9},{9,13},{13,1},{2,6},{6,10},{... | collective-permute-start | bytes 442376 | tf_op jit(solution)/shard_map/ppermute | solution.py:118
  386.6 19.2 %collective-permute-start.28 = (bf16[192,384]{0,1:T(8,128)(2,1)S(1)}, bf16[192,384]{0,1:T(8,128)(2,1)S(1)}, u32[]{:S(2)}, u32[]{:S(2)}) collective-permute-start(bf16[192,384]{0,1:T(8,128)(2,1)S(1)} %get-tuple-element.321), channel_id=1, source_target_pairs={{0,12},{4,0},{8,4},{12,8},{1,13},{5,1},{9,5},{13,9},{2,14},{6,2},{... | collective-permute-start | bytes 442376 | tf_op jit(solution)/shard_map/ppermute | solution.py:118
  398.8 16.9 %collective-permute-start.27 = (bf16[192,384]{0,1:T(8,128)(2,1)S(1)}, bf16[192,384]{0,1:T(8,128)(2,1)S(1)}, u32[]{:S(2)}, u32[]{:S(2)}) collective-permute-start(bf16[192,384]{0,1:T(8,128)(2,1)S(1)} %get-tuple-element.322), channel_id=1, source_target_pairs={{0,8},{4,12},{8,0},{12,4},{1,9},{5,13},{9,1},{13,5},{2,10},{6,14},... | collective-permute-start | bytes 442376 | tf_op jit(solution)/shard_map/ppermute | solution.py:118
  399.0 16.9 %collective-permute-start.37 = (bf16[1,192,384]{1,2,0:T(8,128)(2,1)S(1)}, bf16[1,192,384]{1,2,0:T(8,128)(2,1)S(1)}, u32[]{:S(2)}, u32[]{:S(2)}) collective-permute-start(bf16[1,192,384]{1,2,0:T(8,128)(2,1)S(1)} %fusion.86), channel_id=1, source_target_pairs={{0,1},{1,0},{2,3},{3,2},{4,5},{5,4},{6,7},{7,6},{8,9},{9,8},{10,11... | collective-permute-start | bytes 442376 | tf_op jit(solution)/shard_map/ppermute | solution.py:88
  399.6 16.5 %collective-permute-start.18 = (bf16[192,384]{0,1:T(8,128)(2,1)S(1)}, bf16[192,384]{0,1:T(8,128)(2,1)S(1)}, u32[]{:S(2)}, u32[]{:S(2)}) collective-permute-start(bf16[192,384]{0,1:T(8,128)(2,1)S(1)} %get-tuple-element.323), channel_id=1, source_target_pairs={{0,4},{4,8},{8,12},{12,0},{1,5},{5,9},{9,13},{13,1},{2,6},{6,10},{... | collective-permute-start | bytes 442376 | tf_op jit(solution)/shard_map/ppermute | solution.py:118
  405.8 13.9 %collective-permute-start.20 = (bf16[192,384]{0,1:T(8,128)(2,1)S(1)}, bf16[192,384]{0,1:T(8,128)(2,1)S(1)}, u32[]{:S(2)}, u32[]{:S(2)}) collective-permute-start(bf16[192,384]{0,1:T(8,128)(2,1)S(1)} %get-tuple-element.324), channel_id=1, source_target_pairs={{0,12},{4,0},{8,4},{12,8},{1,13},{5,1},{9,5},{13,9},{2,14},{6,2},{... | collective-permute-start | bytes 442376 | tf_op jit(solution)/shard_map/ppermute | solution.py:118
  415.7 12.5 %collective-permute-start.19 = (bf16[192,384]{0,1:T(8,128)(2,1)S(1)}, bf16[192,384]{0,1:T(8,128)(2,1)S(1)}, u32[]{:S(2)}, u32[]{:S(2)}) collective-permute-start(bf16[192,384]{0,1:T(8,128)(2,1)S(1)} %get-tuple-element.325), channel_id=1, source_target_pairs={{0,8},{4,12},{8,0},{12,4},{1,9},{5,13},{9,1},{13,5},{2,10},{6,14},... | collective-permute-start | bytes 442376 | tf_op jit(solution)/shard_map/ppermute | solution.py:118
  415.9 12.6 %collective-permute-start.29 = (bf16[1,192,384]{1,2,0:T(8,128)(2,1)S(1)}, bf16[1,192,384]{1,2,0:T(8,128)(2,1)S(1)}, u32[]{:S(2)}, u32[]{:S(2)}) collective-permute-start(bf16[1,192,384]{1,2,0:T(8,128)(2,1)S(1)} %fusion.85), channel_id=1, source_target_pairs={{0,1},{1,0},{2,3},{3,2},{4,5},{5,4},{6,7},{7,6},{8,9},{9,8},{10,11... | collective-permute-start | bytes 442376 | tf_op jit(solution)/shard_map/ppermute | solution.py:88
  416.1 83.4 %collective-permute-start.38 = (bf16[2,192,384]{1,2,0:T(8,128)(2,1)S(1)}, bf16[2,192,384]{1,2,0:T(8,128)(2,1)S(1)}, u32[]{:S(2)}, u32[]{:S(2)}) collective-permute-start(bf16[2,192,384]{1,2,0:T(8,128)(2,1)S(1)} %maximum_select_fusion.7), channel_id=1, source_target_pairs={{0,2},{1,3},{2,0},{3,1},{4,6},{5,7},{6,4},{7,5},{8,10},{9,11},{10,... | collective-permute-start | bytes 884744 | tf_op jit(solution)/shard_map/ppermute | solution.py:92
  428.4 70.9 %collective-permute-start.21 = (bf16[1,192,384]{1,2,0:T(8,128)(2,1)S(1)}, bf16[1,192,384]{1,2,0:T(8,128)(2,1)S(1)}, u32[]{:S(2)}, u32[]{:S(2)}) collective-permute-start(bf16[1,192,384]{1,2,0:T(8,128)(2,1)S(1)} %fusion.84), channel_id=1, source_target_pairs={{0,1},{1,0},{2,3},{3,2},{4,5},{5,4},{6,7},{7,6},{8,9},{9,8},{10,11... | collective-permute-start | bytes 442376 | tf_op jit(solution)/shard_map/ppermute | solution.py:88
  428.6 72.7 %collective-permute-start.30 = (bf16[2,192,384]{1,2,0:T(8,128)(2,1)S(1)}, bf16[2,192,384]{1,2,0:T(8,128)(2,1)}, u32[]{:S(2)}, u32[]{:S(2)}) collective-permute-start(bf16[2,192,384]{1,2,0:T(8,128)(2,1)S(1)} %maximum_select_fusion.6), channel_id=1, source_target_pairs={{0,2},{1,3},{2,0},{3,1},{4,6},{5,7},{6,4},{7,5},{8,10},{9,11},{10,... | collective-permute-start | bytes 884744 | tf_op jit(solution)/shard_map/ppermute | solution.py:92
  (56 other events, 648.8 us)
